TPU v7x, 256 devices: a whole 4x4x8 slice. The times are simulated.
256 devices in a mesh: row: 64 (over y, z, x_hi), col: 4 (over x_lo, core).
Axes of the slice: x: 4 (x_hi: 2, x_lo: 2; x = x_hi * 2 + x_lo), y: 4, z: 8, core: 2. Of those that a mesh axis runs over, the one named last changes fastest.
Arguments:
- matrix_slab: float32 [16384, 2048], P('row', 'col'), may hold values from -6 to 6
- sketch_matrix: float32 [144, 16384], P(None, 'row'), may hold values from -0.046875 to 0.046875
- pivots: int32 [1, 128], replicated, may hold values from 128 to 1919, as said below
Outputs:
- sketches: float32 [1, 144, 2048], P(None, None, 'col')
- q_panels: float32 [1, 16384, 128], P(None, 'row')
- r_factors: float32 [1, 128, 2048], P(None, None, 'col')
- first_factors: float32 [1, 128, 128], replicated
- slab_out: float32 [16384, 2048], P('row', 'col')
Inputs may be any that keep to these rules, and one draw needn't show every extreme that they name: `pivots`: each row holds 128 different numbers.
All inputs are finite; a program needn't handle non-finite values.
Results may differ from a plain program's by a relative error of at most 0.0003.
Values sent between devices are 32-bit elements; how exact they have to be, the bound alone decides.
A program may use at most 64 MiB of HBM per device.

v0:
```python
import math

import jax
import jax.numpy as jnp
from jax import lax
from jax.sharding import PartitionSpec as P

PANEL = 128


def product(left, right):
    return jnp.dot(left, right, precision=lax.Precision.HIGHEST, preferred_element_type=jnp.float32)


def solve_right(lower, rhs):
    return lax.linalg.triangular_solve(lower, rhs, left_side=False, lower=True, transpose_a=True)


def pick_columns(array, local_ids, inside):
    width = array.shape[1]
    picked = jnp.take(array, jnp.clip(local_ids, 0, width - 1), axis=1)
    return jnp.where(inside[None, :], picked, jnp.float32(0.0))


def place_columns(array, local_ids, inside, values):
    target = jnp.where(inside, local_ids, array.shape[1])
    return array.at[:, target].set(values, mode="drop")


def shards(matrix_slab, sketch_matrix, pivots):
    rows_dev, col_width = matrix_slab.shape
    m_total = rows_dev * lax.axis_size("row")
    row_scale = math.sqrt(m_total)
    col_first = lax.axis_index("col") * col_width
    column = col_first + jnp.arange(col_width, dtype=jnp.int32)
    current = matrix_slab
    sketch = lax.psum(product(sketch_matrix, current), "row")
    sketch_list = [sketch]
    pivot_ids = 0 + pivots[0]
    slot_ids = 0 + jnp.arange(PANEL, dtype=jnp.int32)
    pivot_local = pivot_ids - col_first
    slot_local = slot_ids - col_first
    pivot_inside = (pivot_local >= 0) & (pivot_local < col_width)
    slot_inside = (slot_local >= 0) & (slot_local < col_width)
    in_slots = (column >= 0) & (column < PANEL)
    panel_cols, lead_cols = lax.psum(
        (
            pick_columns(current, pivot_local, pivot_inside),
            pick_columns(current, slot_local, slot_inside),
        ),
        "col",
    )
    swapped = place_columns(
        place_columns(current, slot_local, slot_inside, panel_cols),
        pivot_local,
        pivot_inside,
        lead_cols,
    )
    gram_one = lax.psum(product(panel_cols.T, panel_cols), "row")
    factor_one = jnp.linalg.cholesky(gram_one)
    basis_one = solve_right(factor_one, panel_cols)
    gram_two = lax.psum(product(basis_one.T, basis_one), "row")
    factor_two = jnp.linalg.cholesky(gram_two)
    basis = solve_right(factor_two, basis_one)
    r_factor = product(factor_two.T, factor_one.T)
    projected = lax.psum(product(basis.T, swapped), "row")
    r_block = place_columns(projected, slot_local, slot_inside, r_factor)
    current = jnp.where(in_slots[None, :], jnp.float32(0.0), swapped - product(basis, projected))
    q_list = [basis * row_scale]
    r_list = [r_block / row_scale]
    first_list = [factor_one.T / row_scale]
    return (
        jnp.stack(sketch_list),
        jnp.stack(q_list),
        jnp.stack(r_list),
        jnp.stack(first_list),
        current,
    )


def solution(mesh):
    in_specs = (P("row", "col"), P(None, "row"), P())
    out_specs = (
        P(None, None, "col"),
        P(None, "row", None),
        P(None, None, "col"),
        P(),
        P("row", "col"),
    )
    return jax.shard_map(shards, mesh=mesh, in_specs=in_specs, out_specs=out_specs, check_vma=False)
```

profile of v0, /device:TPU:1, one launch (start us, length us, event | category | flops | bytes accessed | tf_op | source)
XLA Modules:
  0.0 1970.0 jit_solution(17937217708790303102)
XLA Ops:
  8.0 1.2 copy.8
  10.8 0.8 bitcast_select_fusion.1
  11.5 0.8 bitcast_select_fusion
  12.4 45.8 %all-reduce.13.cloned.1.call-done = (f32[256,128]{0,1:T(8,128)}, f32[256,128]{0,1:T(8,128)}) async-done(((f32[256,128]{0,1:T(8,128)}, f32[256,128]{0,1:T(8,128)}), (f32[256,128]{0,1:T(8,128)}, f32[256,128]{0,1:T(8,128)})) %all-reduce.13.cloned.1.call-update) | async-done | bytes 262160 | tf_op jit(solution)/shard_map/psum | solution.py:46
  58.2 1.9 fusion.29
  60.2 587.7 %all-reduce.7.cloned.1.call-done = f32[128,128]{0,1:T(8,128)} async-done(((f32[128,128]{0,1:T(8,128)}), f32[128,128]{0,1:T(8,128)}) %all-reduce.7.cloned.1.call-update) | async-done | bytes 65552 | tf_op jit(solution)/shard_map/psum | solution.py:59
  647.9 1.0 copy.10
  648.9 11.7 cholesky.44
  662.0 9.8 custom-call.6
  672.1 0.9 fusion.30
  673.1 1.2 convolution_bitcast_fusion
  674.3 1.2 scatter_custom_fusion
  675.5 1.4 scatter_custom_fusion.1
  677.0 610.2 %all-reduce.9.cloned.1.call-done = f32[128,128]{0,1:T(8,128)} async-done(((f32[128,128]{0,1:T(8,128)}), f32[128,128]{0,1:T(8,128)}) %all-reduce.9.cloned.1.call-update) | async-done | bytes 65552 | tf_op jit(solution)/shard_map/psum | solution.py:62
  1287.2 1.0 copy.12
  1288.2 11.7 cholesky.55
  1301.4 9.8 custom-call.7
  1311.5 1.3 fusion.31
  1314.6 1.5 fusion.15
  1316.1 642.2 %all-reduce.11.cloned.1.call-done = (f32[1,144,512]{2,1,0:T(8,128)}, f32[128,512]{1,0:T(8,128)}) async-done(((f32[1,144,512]{2,1,0:T(8,128)}, f32[128,512]{1,0:T(8,128)}), (f32[1,144,512]{2,1,0:T(8,128)}, f32[128,512]{1,0:T(8,128)})) %all-reduce.11.cloned.1.call-update) | async-done | bytes 557072 | tf_op jit(solution)/shard_map/psum | solution.py:37
  1958.2 1.1 copy.15
  1959.3 1.0 scatter_fusion
  1960.4 0.8 copy.18
  1961.3 1.4 fusion
  (52 shorter events, 8.4 us)
Async XLA Ops:
  7.2 665.9 %copy-start = (f32[144,256]{1,0:T(8,128)S(1)}, f32[144,256]{1,0:T(8,128)}, u32[]{:S(2)}) copy-start(f32[144,256]{1,0:T(8,128)} %param.9) | copy-start | bytes 442372
  7.2 51.0 %all-reduce.13.cloned.1.call-start = ((), (), s32[]{:S(2)}) async-start(), calls=%async_computation.3 | async-start | bytes 524288 | tf_op jit(solution)/shard_map/psum | solution.py:46
  7.2 0.7 copy-start.8
  12.3 635.6 %all-reduce.7.cloned.1.call-start = ((), (), s32[]{:S(2)}) async-start(), calls=%async_computation | async-start | bytes 131072 | tf_op jit(solution)/shard_map/psum | solution.py:59
  60.1 1227.1 %all-reduce.9.cloned.1.call-start = ((), (), s32[]{:S(2)}) async-start(), calls=%async_computation.1 | async-start | bytes 131072 | tf_op jit(solution)/shard_map/psum | solution.py:62
  647.9 1.0 copy-start.6
  660.6 11.2 copy-start.1
  660.6 12.5 copy-start.2
  673.0 1285.2 %all-reduce.11.cloned.1.call-start = ((), (), s32[]{:S(2)}) async-start(), calls=%async_computation.2 | async-start | bytes 1114112 | tf_op jit(solution)/shard_map/psum | solution.py:37
  674.3 1.2 copy-start.7
  1287.2 1.0 copy-start.5
  1960.4 1.0 copy-start.3
  1961.3 1.4 copy-start.4
Sparse Core Ops, SparseCore 0:
  12.4 45.7 all-reduce.12
  61.6 586.2 all-reduce.6
  673.2 613.9 all-reduce.8
  1313.0 645.2 all-reduce.10
where the time goes:
time: 2000 us; the launch traced here: 1970 us
  waiting for transfers between devices  1890 us (94%)
  other arithmetic  47.4 us (2%)
    psum x1, waiting for transfers between devices, shards(): sketch = lax.psum(product(sketch_matrix, current), 'row')  642 us
    psum x1, waiting for transfers between devices, shards(): gram_two = lax.psum(product(basis_one.T, basis_one), 'row')  610 us
    psum x1, waiting for transfers between devices, shards(): gram_one = lax.psum(product(panel_cols.T, panel_cols), 'row')  588 us
    psum x1, waiting for transfers between devices, shards(): lax.psum((pick_columns(current, pivot_local, pivot_inside), pick_columns(...  45.8 us
  transfers between devices with their start and end apart: 4, of which 4 were waited for; matrix products, arithmetic and copies ran while one was open for 0% of the time, Pallas kernels for 0%

commit v1 on v0

v1 whole, which is shorter than its diff:
```python
import functools
import math

import jax
import jax.numpy as jnp
from jax import lax
from jax.experimental import pallas as pl
from jax.experimental.pallas import tpu as pltpu
from jax.sharding import PartitionSpec as P

PANEL = 128
NYX = 8
NZ = 8
NCOL = 4
MESH = pl.DeviceIdType.MESH
F32 = jnp.float32
BF16 = jnp.bfloat16
VMEM_SPEC = pl.BlockSpec(memory_space=pltpu.VMEM)


def hdot(left, right, contract=(1, 0)):
    return lax.dot_general(
        left,
        right,
        (((contract[0],), (contract[1],)), ((), ())),
        precision=lax.Precision.HIGHEST,
        preferred_element_type=F32,
    )


def bdot(left, right, contract=(1, 0)):
    return lax.dot_general(
        left, right, (((contract[0],), (contract[1],)), ((), ())), preferred_element_type=F32
    )


def select_dot(values, onehot, contract=(1, 0)):
    high = values.astype(BF16)
    rest = values - high.astype(F32)
    mid = rest.astype(BF16)
    low = (rest - mid.astype(F32)).astype(BF16)
    return (bdot(high, onehot, contract) + bdot(mid, onehot, contract)) + bdot(low, onehot, contract)


def two_sum(a, b):
    s = a + b
    t = s - a
    return s, (a - (s - t)) + (b - t)


def gram_levels(x):
    n = x.shape[1]
    sigma = jnp.max(jnp.abs(x), axis=0, keepdims=True) * 131072.0
    parts = []
    rest = x
    for _ in range(4):
        part = (rest + sigma) - sigma
        rest = rest - part
        parts.append(part.astype(BF16))
        sigma = sigma * (1.0 / 128.0)
    cat = jnp.concatenate(parts, axis=1)
    full = bdot(cat, cat, (0, 0))
    block = lambda i, j: full[i * n : (i + 1) * n, j * n : (j + 1) * n]
    return (
        block(0, 0),
        block(0, 1) + block(1, 0),
        (block(0, 2) + block(2, 0)) + block(1, 1),
        (block(0, 3) + block(3, 0)) + (block(1, 2) + block(2, 1)),
        (block(1, 3) + block(3, 1)) + block(2, 2),
    )


def pivot_onehot(piv, col_first, width):
    lanes = lax.broadcasted_iota(jnp.int32, (width, PANEL), 0) + col_first
    return jnp.where(lanes == piv, 1.0, 0.0).astype(BF16)


def swapped_columns(slab, lead, onehot):
    picked = bdot(jnp.ones((8, PANEL), BF16), onehot, (1, 1))[0:1, :]
    return jnp.where(picked > 0.5, select_dot(lead, onehot, (1, 1)), slab)


def remote(src, dst, send, recv, device):
    return pltpu.make_async_remote_copy(
        src_ref=src, dst_ref=dst, send_sem=send, recv_sem=recv, device_id=device, device_id_type=MESH
    )


def gather_kernel(
    slab_ref, sketch_ref, piv_ref,
    p_ref, lead_ref, g_ref, hi_ref, lo_ref, s_ref,
    pk, pp, rc1, rc2, leadbuf,
    wpart, wa, wsum, wb, wfull,
    gpart, ga, gsum, gb, gfull,
    spart, sa, ssum, sb, sb9, sfull,
    sem1, sem_lead, wa_sem, wb_sem, wc_sem, ga_sem, gb_sem, gc_sem, gd_sem,
    sa_sem, sb_sem, sb9_sem, sc_sem, sd_sem,
):
    r = lax.axis_index("row")
    c = lax.axis_index("col")
    z = lax.rem(lax.div(r, 2), NZ)
    q = lax.div(r, 16) * 2 + lax.rem(r, 2)
    width = slab_ref.shape[1]

    def yx_row(t):
        return lax.div(t, 2) * 16 + z * 2 + lax.rem(t, 2)

    def z_row(t):
        return lax.div(r, 16) * 16 + t * 2 + lax.rem(r, 2)

    barrier = pltpu.get_barrier_semaphore()
    for i in range(NYX):
        for j in range(NCOL):
            if i or j:
                pl.semaphore_signal(
                    barrier, inc=1, device_id_type=MESH,
                    device_id=(yx_row(lax.rem(q + i, NYX)), lax.rem(c + j, NCOL)),
                )
    for i in range(1, NZ):
        pl.semaphore_signal(
            barrier, inc=1, device_id=(z_row(lax.rem(z + i, NZ)), c), device_id_type=MESH
        )

    slab = slab_ref[...]
    onehot = pivot_onehot(piv_ref[...], c * width, width)
    pk[...] = select_dot(slab, onehot)
    pl.semaphore_wait(barrier, NYX * NCOL - 1 + NZ - 1)

    core = c + 1 - 2 * lax.rem(c, 2)
    chip = lax.rem(c + 2, NCOL)
    first = remote(pk, rc1, sem1.at[0], sem1.at[1], (r, core))
    first.start()
    sketch = hdot(sketch_ref[...], slab)
    for b in range(4):
        spart[18 * b : 18 * b + 18] = sketch[:, 128 * b : 128 * b + 128].reshape(18, 8, 128)
    first.wait_recv()
    pp[...] = pk[...] + rc1[...]
    second = remote(pp, rc2, sem1.at[2], sem1.at[3], (r, chip))
    second.start()

    lead_copies = [
        remote(leadbuf.at[0], leadbuf.at[1], sem_lead.at[j - 1], sem_lead.at[3], (r, j)) for j in range(1, NCOL)
    ]
    leadbuf[0] = slab[:, :PANEL]

    @pl.when(c == 0)
    def _():
        for copy in lead_copies:
            copy.start()

    second.wait_recv()
    panel = pp[...] + rc2[...]
    p_ref[...] = panel

    lane = lax.broadcasted_iota(jnp.int32, (PANEL, PANEL), 1)
    l0, l1, l2, l3, l4 = gram_levels(panel)
    high, low = two_sum(l0, l1)
    high, low2 = two_sum(high, l2)
    low = (low + low2) + (l3 + l4)
    left = lane < 64
    wpart[0:16] = jnp.where(left, high, pltpu.roll(low, 64, 1)).reshape(16, 8, 128)
    wpart[16:32] = jnp.where(left, pltpu.roll(high, 64, 1), low).reshape(16, 8, 128)

    pending = [first, second]

    def exchange(me, count, row_of, src, dst, send_sems, recv_sems):
        copies = []
        for i in range(1, count):
            t = lax.rem(me + i, count)
            copy = remote(src(t), dst(me), send_sems.at[t], recv_sems.at[me], (row_of(t), c))
            copy.start()
            copies.append(copy)
        pending.extend(copies)

    def arrived(me, count, dst, send_sems, recv_sems):
        for i in range(1, count):
            t = lax.rem(me + i, count)
            remote(dst(t), dst(t), send_sems.at[t], recv_sems.at[t], (r, c)).wait_recv()

    yx = functools.partial(exchange, q, NYX, yx_row)
    zz = functools.partial(exchange, z, NZ, z_row)

    def two_float_total(buf):
        total = buf[0]
        err = jnp.zeros((8, 128), F32)
        for k in range(1, 8):
            total, e = two_sum(total, buf[k])
            err = err + e
        lane8 = lax.broadcasted_iota(jnp.int32, (8, 128), 1)
        return jnp.where(lane8 < 64, total, total + pltpu.roll(err, 64, 1))

    yx(lambda t: wpart.at[c * 8 + t], lambda m: wa.at[m], wa_sem.at[0], wa_sem.at[1])
    yx(
        lambda t: spart.at[pl.ds(9 * t, 9)], lambda m: sa.at[m], sa_sem.at[0], sa_sem.at[1]
    )
    wa[q] = wpart[c * 8 + q]
    sa[q] = spart[pl.ds(9 * q, 9)]

    @pl.when(c != 0)
    def _():
        remote(leadbuf.at[0], leadbuf.at[1], sem_lead.at[0], sem_lead.at[3], (r, c)).wait_recv()

    lead = jnp.where(c == 0, leadbuf[0], leadbuf[1])
    lead_ref[...] = lead
    swapped = swapped_columns(slab, lead, onehot)
    inner = hdot(panel, swapped, (0, 0))
    for b in range(4):
        gpart[16 * b : 16 * b + 16] = inner[:, 128 * b : 128 * b + 128].reshape(16, 8, 128)

    arrived(q, NYX, lambda t: wa.at[t], wa_sem.at[0], wa_sem.at[1])
    wsum[0] = two_float_total(wa)
    zz(lambda t: wsum.at[0], lambda m: wb.at[m], wb_sem.at[0], wb_sem.at[1])
    yx(lambda t: gpart.at[pl.ds(8 * t, 8)], lambda m: ga.at[m], ga_sem.at[0], ga_sem.at[1])
    wb[z] = wsum[0]
    ga[q] = gpart[pl.ds(8 * q, 8)]

    arrived(q, NYX, lambda t: sa.at[t], sa_sem.at[0], sa_sem.at[1])
    total = sa[0]
    for k in range(1, NYX):
        total = total + sa[k]
    ssum[...] = total
    zz(lambda t: ssum.at[t], lambda m: sb.at[m], sb_sem.at[0], sb_sem.at[1])
    zz(lambda t: ssum.at[8], lambda m: sb9.at[m], sb9_sem.at[0], sb9_sem.at[1])
    sb[z] = ssum[z]
    sb9[z] = ssum[8]

    arrived(z, NZ, lambda t: wb.at[t], wb_sem.at[0], wb_sem.at[1])
    mine = c * 8 + q
    wsum[1] = two_float_total(wb)
    for i in range(NYX):
        for j in range(NCOL):
            if i or j:
                t = lax.rem(q + i, NYX)
                d = lax.rem(c + j, NCOL)
                copy = remote(
                    wsum.at[1], wfull.at[mine], wc_sem.at[0, d * 8 + t], wc_sem.at[1, mine], (yx_row(t), d)
                )
                copy.start()
                pending.append(copy)
    wfull[mine] = wsum[1]

    arrived(q, NYX, lambda t: ga.at[t], ga_sem.at[0], ga_sem.at[1])
    total = ga[0]
    for k in range(1, NYX):
        total = total + ga[k]
    gsum[...] = total
    zz(lambda t: gsum.at[t], lambda m: gb.at[m], gb_sem.at[0], gb_sem.at[1])
    gb[z] = gsum[z]

    arrived(z, NZ, lambda t: sb.at[t], sb_sem.at[0], sb_sem.at[1])
    arrived(z, NZ, lambda t: sb9.at[t], sb9_sem.at[0], sb9_sem.at[1])
    total, ninth = sb[0], sb9[0]
    for k in range(1, NZ):
        total = total + sb[k]
        ninth = ninth + sb9[k]
    sfull[q * 9 + z] = total
    sfull[q * 9 + 8] = ninth
    zz(
        lambda t: sfull.at[q * 9 + z], lambda m: sfull.at[q * 9 + m], sc_sem.at[0], sc_sem.at[1]
    )

    arrived(z, NZ, lambda t: gb.at[t], gb_sem.at[0], gb_sem.at[1])
    total = gb[0]
    for k in range(1, NZ):
        total = total + gb[k]
    gfull[q * 8 + z] = total
    zz(
        lambda t: gfull.at[q * 8 + z], lambda m: gfull.at[q * 8 + m], gc_sem.at[0], gc_sem.at[1]
    )

    arrived(z, NZ, lambda t: sfull.at[q * 9 + t], sc_sem.at[0], sc_sem.at[1])
    yx(
        lambda t: sfull.at[pl.ds(q * 9, 9)], lambda m: sfull.at[pl.ds(m * 9, 9)], sd_sem.at[0], sd_sem.at[1]
    )
    arrived(z, NZ, lambda t: gfull.at[q * 8 + t], gc_sem.at[0], gc_sem.at[1])
    yx(
        lambda t: gfull.at[pl.ds(q * 8, 8)], lambda m: gfull.at[pl.ds(m * 8, 8)], gd_sem.at[0], gd_sem.at[1]
    )

    for i in range(NYX):
        for j in range(NCOL):
            if i or j:
                o = lax.rem(c + j, NCOL) * 8 + lax.rem(q + i, NYX)
                remote(wfull.at[o], wfull.at[o], wc_sem.at[0, o], wc_sem.at[1, o], (r, c)).wait_recv()
    first_half = wfull[0:16].reshape(PANEL, PANEL)
    second_half = wfull[16:32].reshape(PANEL, PANEL)
    hi_ref[...] = jnp.where(left, first_half, pltpu.roll(second_half, 64, 1))
    lo_ref[...] = jnp.where(left, pltpu.roll(first_half, 64, 1), second_half)

    arrived(q, NYX, lambda t: sfull.at[pl.ds(t * 9, 9)], sd_sem.at[0], sd_sem.at[1])
    for b in range(4):
        s_ref[0, :, 128 * b : 128 * b + 128] = sfull[18 * b : 18 * b + 18].reshape(144, 128)
    arrived(q, NYX, lambda t: gfull.at[pl.ds(t * 8, 8)], gd_sem.at[0], gd_sem.at[1])
    for b in range(4):
        g_ref[:, 128 * b : 128 * b + 128] = gfull[16 * b : 16 * b + 16].reshape(128, 128)

    for copy in pending:
        copy.wait_send()

    @pl.when(c == 0)
    def _():
        for copy in lead_copies:
            copy.wait_send()


def eliminate(aug):
    sub = lax.broadcasted_iota(jnp.int32, (8, 2 * PANEL), 0)
    sub1 = lax.broadcasted_iota(jnp.int32, (8, 1), 0)
    for b in range(PANEL // 8):
        rows = aug[8 * b : 8 * b + 8, :]
        for i in range(8):
            at = 8 * b + i
            column = rows[:, at : at + 1]
            inv = lax.rsqrt(column[i : i + 1, :])
            pivot_row = rows[i : i + 1, :] * inv
            coef = jnp.where(sub1 > i, column * inv, 0.0)
            rows = jnp.where(sub == i, pivot_row, rows - coef * pivot_row)
        aug[8 * b : 8 * b + 8, :] = rows
        if b < PANEL // 8 - 1:
            update = hdot(rows[:, :PANEL], rows, (0, 0))
            aug[8 * b + 8 :, :] = aug[8 * b + 8 :, :] - update[8 * b + 8 :, :]


def factor_kernel(
    slab_ref, piv_ref, p_ref, lead_ref, g_ref, hi_ref, lo_ref,
    q_ref, r_ref, first_ref, out_ref, aug,
):
    c = lax.axis_index("col")
    width = slab_ref.shape[1]
    rowi = lax.broadcasted_iota(jnp.int32, (PANEL, PANEL), 0)
    coli = lax.broadcasted_iota(jnp.int32, (PANEL, PANEL), 1)
    eye = jnp.where(rowi == coli, 1.0, 0.0).astype(F32)
    upper = coli >= rowi
    lower = coli <= rowi
    scale = 1.0 / 128.0

    high = hi_ref[...]
    aug[:, :PANEL] = high
    aug[:, PANEL:] = eye
    eliminate(aug)
    r_one = jnp.where(upper, aug[:, :PANEL], 0.0)
    x_one = jnp.where(lower, aug[:, PANEL:], 0.0)
    first_ref[0] = r_one * scale

    l0, l1, l2, l3, l4 = gram_levels(r_one)
    d, e1 = two_sum(high, -l0)
    d, e2 = two_sum(d, -l1)
    delta = (d - l2) + (((e1 + e2) + lo_ref[...]) - (l3 + l4))
    gram_two = eye + hdot(hdot(x_one, delta), x_one, (1, 1))
    aug[:, :PANEL] = gram_two
    aug[:, PANEL:] = eye
    eliminate(aug)
    r_two = jnp.where(upper, aug[:, :PANEL], 0.0)
    x_two = jnp.where(lower, aug[:, PANEL:], 0.0)
    r_factor = hdot(r_two, r_one)

    slab = slab_ref[...]
    onehot = pivot_onehot(piv_ref[...], c * width, width)
    swapped = swapped_columns(slab, lead_ref[...], onehot)
    basis = hdot(hdot(p_ref[...], x_one, (1, 1)), x_two, (1, 1))
    projected = hdot(x_two, hdot(x_one, g_ref[...]))
    q_ref[0] = basis * 128.0
    lead_block = c == 0
    r_ref[0, :, :PANEL] = jnp.where(lead_block, r_factor, projected[:, :PANEL]) * scale
    r_ref[0, :, PANEL:] = projected[:, PANEL:] * scale
    rest = swapped - hdot(basis, projected)
    out_ref[:, :PANEL] = jnp.where(lead_block, 0.0, rest[:, :PANEL])
    out_ref[:, PANEL:] = rest[:, PANEL:]


def shards(matrix_slab, sketch_matrix, pivots):
    rows, width = matrix_slab.shape
    sk = sketch_matrix.shape[0]
    dma = pltpu.SemaphoreType.DMA
    tile = lambda *lead: pltpu.VMEM(lead + (8, 128), F32)
    flat = lambda *shape: jax.ShapeDtypeStruct(shape, F32)
    panel, lead, inner, high, low, sketches = pl.pallas_call(
        gather_kernel,
        out_shape=(
            flat(rows, PANEL), flat(rows, PANEL), flat(PANEL, width),
            flat(PANEL, PANEL), flat(PANEL, PANEL), flat(1, sk, width),
        ),
        in_specs=[VMEM_SPEC] * 3,
        out_specs=(VMEM_SPEC,) * 6,
        scratch_shapes=[
            pltpu.VMEM((rows, PANEL), F32), pltpu.VMEM((rows, PANEL), F32),
            pltpu.VMEM((rows, PANEL), F32), pltpu.VMEM((rows, PANEL), F32),
            pltpu.VMEM((2, rows, PANEL), F32),
            tile(32), tile(8), tile(2), tile(8), tile(32),
            tile(64), tile(8, 8), tile(8), tile(8), tile(64),
            tile(72), tile(8, 9), tile(9), tile(8), tile(8), tile(72),
            dma((4,)), dma((4,)), dma((2, 8)), dma((2, 8)), dma((2, 32)),
            dma((2, 8)), dma((2, 8)), dma((2, 8)), dma((2, 8)),
            dma((2, 8)), dma((2, 8)), dma((2, 8)), dma((2, 8)), dma((2, 8)),
        ],
        compiler_params=pltpu.CompilerParams(
            collective_id=0, has_side_effects=True, vmem_limit_bytes=32 * 1024 * 1024
        ),
        name="gather",
    )(matrix_slab, sketch_matrix, pivots)
    q_panels, r_factors, first, slab_out = pl.pallas_call(
        factor_kernel,
        out_shape=(
            flat(1, rows, PANEL), flat(1, PANEL, width), flat(1, PANEL, PANEL), flat(rows, width),
        ),
        in_specs=[VMEM_SPEC] * 7,
        out_specs=(VMEM_SPEC,) * 4,
        scratch_shapes=[pltpu.VMEM((PANEL, 2 * PANEL), F32)],
        compiler_params=pltpu.CompilerParams(vmem_limit_bytes=32 * 1024 * 1024),
        name="factor",
    )(matrix_slab, pivots, panel, lead, inner, high, low)
    return sketches, q_panels, r_factors, first, slab_out


def solution(mesh):
    in_specs = (P("row", "col"), P(None, "row"), P())
    out_specs = (
        P(None, None, "col"),
        P(None, "row", None),
        P(None, None, "col"),
        P(),
        P("row", "col"),
    )
    return jax.shard_map(shards, mesh=mesh, in_specs=in_specs, out_specs=out_specs, check_vma=False)
```

time: 2000 us -> 82.6 us (0.04); the launches traced: 1970 us -> 81.3 us
  waiting for transfers between devices: 1890 us -> 0 us
  Pallas kernels: 0 us -> 77.3 us
  other arithmetic: 47.4 us -> 0 us
    psum x4 -> x0, waiting for transfers between devices: 1890 us -> none  [the longest x1 642 us: shards(): sketch = lax.psum(product(sketch_matrix, current), 'row')]
    pallas_call x0 -> x2, Pallas kernels: none -> 77.3 us  [the longest x1 42.6 us: shards(): pl.pallas_call(gather_kernel, out_shape=(flat(rows, PANEL), flat(rows, PA...]
    another operation x12 -> x0, other arithmetic: 45.8 us -> none  [the longest x3 20.3 us: solve_right(): lax.linalg.triangular_solve(lower, rhs, left_side=False, lower=True, tran...]
  transfers between devices with their start and end apart: 4 -> 0, of which waited for: 4 -> 0; matrix products, arithmetic and copies ran while one was open for 0% -> 0% of each run, Pallas kernels for 0% -> 0%
where the time goes in v1:
time: 82.6 us; the launch traced here: 81.3 us
  Pallas kernels  77.3 us (94%)
  local copies, waits for them, and re-layouts  3.31 us (4%)
    pallas_call x1, Pallas kernels, shards(): pl.pallas_call(gather_kernel, out_shape=(flat(rows, PANEL), flat(rows, PA...  42.6 us
    pallas_call x1, Pallas kernels, shards(): pl.pallas_call(factor_kernel, out_shape=(flat(1, rows, PANEL), flat(1, PA...  34.7 us
    unnamed x7, local copies, waits for them, and re-layouts  3.31 us

profile of v1, /device:TPU:1, one launch (start us, length us, event | category | flops | bytes accessed | tf_op | source)
XLA Modules:
  0.0 81.3 jit_solution(9094871516110786541)
XLA Ops:
  0.6 0.0 copy-start
  0.6 1.0 %copy-done = f32[256,512]{1,0:T(8,128)S(1)} copy-done((f32[256,512]{1,0:T(8,128)S(1)}, f32[256,512]{1,0:T(8,128)}, u32[]{:S(2)}) %copy-start) | copy-done | bytes 524312
  1.7 0.0 copy-start.1
  1.7 0.9 %copy-done.1 = f32[144,256]{1,0:T(8,128)S(1)} copy-done((f32[144,256]{1,0:T(8,128)S(1)}, f32[144,256]{1,0:T(8,128)}, u32[]{:S(2)}) %copy-start.1) | copy-done | bytes 147480
  2.6 0.0 copy-start.2
  2.6 0.7 copy-done.2
  3.2 42.6 %gather.1 = (f32[256,128]{1,0:T(8,128)S(1)}, f32[256,128]{1,0:T(8,128)S(1)}, f32[128,512]{1,0:T(8,128)S(1)}, f32[128,128]{1,0:T(8,128)S(1)}, f32[128,128]{1,0:T(8,128)S(1)}, /*index=5*/f32[1,144,512]{2,1,0:T(8,128)S(1)}) custom-call(f32[256,512]{1,0:T(8,128)S(1)} %copy-done, f32[144,256]{1,0:T(8,128)S(1)} %copy-done.1, s32[1,128]{1,0:T(1,128)S(1)} %copy-done.2), custom_call_target="tpu_custom_call" | custom-call | tf_op jit(solution)/shard_map/gather/pallas_call | solution.py:377
  45.9 34.7 %factor.1 = (f32[1,256,128]{2,1,0:T(8,128)}, f32[1,128,512]{2,1,0:T(8,128)}, f32[1,128,128]{2,1,0:T(8,128)}, f32[256,512]{1,0:T(8,128)}) custom-call(f32[256,512]{1,0:T(8,128)S(1)} %copy-done, s32[1,128]{1,0:T(1,128)S(1)} %copy-done.2, f32[256,128]{1,0:T(8,128)S(1)} %get-tuple-element.16.p_ref, f32[256,128]{1,0:T(8,128)S(1)} %get-tuple-element.17.lead_ref, ...), custom_call_target="tpu_custom_call" | custom-call | tf_op jit(solution)/shard_map/factor/pallas_call | solution.py:401
  80.6 0.7 copy.9
Async XLA Ops:
  0.6 1.0 %copy-start = (f32[256,512]{1,0:T(8,128)S(1)}, f32[256,512]{1,0:T(8,128)}, u32[]{:S(2)}) copy-start(f32[256,512]{1,0:T(8,128)} %slab_ref.3) | copy-start | bytes 1572868
  1.7 0.9 %copy-start.1 = (f32[144,256]{1,0:T(8,128)S(1)}, f32[144,256]{1,0:T(8,128)}, u32[]{:S(2)}) copy-start(f32[144,256]{1,0:T(8,128)} %sketch_ref.1) | copy-start | bytes 442372
  2.6 0.7 copy-start.2

commit v2 on v1

--- a/solution.py
+++ b/solution.py
@@ -303,43 +303,92 @@
             copy.wait_send()
 
 
-def eliminate(aug):
-    sub = lax.broadcasted_iota(jnp.int32, (8, 2 * PANEL), 0)
-    sub1 = lax.broadcasted_iota(jnp.int32, (8, 1), 0)
-    for b in range(PANEL // 8):
-        rows = aug[8 * b : 8 * b + 8, :]
-        for i in range(8):
-            at = 8 * b + i
-            column = rows[:, at : at + 1]
-            inv = lax.rsqrt(column[i : i + 1, :])
-            pivot_row = rows[i : i + 1, :] * inv
-            coef = jnp.where(sub1 > i, column * inv, 0.0)
-            rows = jnp.where(sub == i, pivot_row, rows - coef * pivot_row)
-        aug[8 * b : 8 * b + 8, :] = rows
-        if b < PANEL // 8 - 1:
-            update = hdot(rows[:, :PANEL], rows, (0, 0))
-            aug[8 * b + 8 :, :] = aug[8 * b + 8 :, :] - update[8 * b + 8 :, :]
+def tree_sum(terms):
+    terms = list(terms)
+    while len(terms) > 1:
+        pairs = [terms[i] + terms[i + 1] for i in range(0, len(terms) - 1, 2)]
+        terms = pairs + terms[len(pairs) * 2 :]
+    return terms[0]
+
+
+def spread(v):
+    return jnp.broadcast_to(v, (8, 128))
+
+
+def block_factor(v, first, sub, lane):
+    columns = [spread(v[:, first + j : first + j + 1]) for j in range(8)]
+    a = {(i, j): spread(columns[i][j : j + 1, :]) for j in range(8) for i in range(j + 1)}
+    m = [[None] * 8 for _ in range(8)]
+    for i in range(8):
+        inv = lax.rsqrt(a[i, i])
+        l = {j: a[i, j] * inv for j in range(i + 1, 8)}
+        for j in range(i + 1, 8):
+            for k in range(j, 8):
+                a[j, k] = a[j, k] - l[j] * l[k]
+        for j in range(i):
+            m[i][j] = m[i][j] * inv
+        m[i][i] = inv
+        for k in range(i + 1, 8):
+            for j in range(i + 1):
+                t = l[k] * m[i][j]
+                m[k][j] = -t if m[k][j] is None else m[k][j] - t
+    terms = []
+    inverse = jnp.zeros((8, 128), F32)
+    for j in range(8):
+        column = m[7][j]
+        for k in range(6, j - 1, -1):
+            column = jnp.where(sub <= k, m[k][j], column)
+        if j > 0:
+            column = jnp.where(sub < j, 0.0, column)
+        terms.append(column * spread(v[j : j + 1, :]))
+        inverse = jnp.where(lane == first + j, column, inverse)
+    solved = tree_sum(terms)
+    inside = (lane >= first) & (lane < first + 8)
+    return solved, jnp.where(inside, inverse, solved), m
+
+
+def eliminate(w, r_ref, x_ref):
+    sub = lax.broadcasted_iota(jnp.int32, (8, 128), 0)
+    lane = lax.broadcasted_iota(jnp.int32, (8, 128), 1)
+    count = PANEL // 8
+    blocks = [w[8 * b : 8 * b + 8, :] for b in range(count)]
+    for b in range(count):
+        first = 8 * b
+        solved, both, m = block_factor(blocks[b], first, sub, lane)
+        upper = jnp.where(lane >= first + sub, solved, 0.0)
+        r_ref[first : first + 8, :] = upper
+        x_ref[first : first + 8, :] = jnp.where(lane < first + 8, both, 0.0)
+        if b == count - 1:
+            break
+        inside = (lane >= first) & (lane < first + 8)
+        rows = blocks[b + 1]
+        columns = [spread(rows[:, first + j : first + j + 1]) for j in range(8)]
+        updates = []
+        for p in range(8):
+            coef = tree_sum([m[p][j] * columns[j] for j in range(p + 1)])
+            updates.append(coef * spread(both[p : p + 1, :]))
+        blocks[b + 1] = jnp.where(inside, 0.0, rows) - tree_sum(updates)
+        if b + 2 < count:
+            update = hdot(upper, both, (0, 0))
+            for k in range(b + 2, count):
+                blocks[k] = jnp.where(inside, 0.0, blocks[k]) - update[8 * k : 8 * k + 8, :]
 
 
 def factor_kernel(
     slab_ref, piv_ref, p_ref, lead_ref, g_ref, hi_ref, lo_ref,
-    q_ref, r_ref, first_ref, out_ref, aug,
+    q_ref, r_ref, first_ref, out_ref, rbuf, xbuf,
 ):
     c = lax.axis_index("col")
     width = slab_ref.shape[1]
     rowi = lax.broadcasted_iota(jnp.int32, (PANEL, PANEL), 0)
     coli = lax.broadcasted_iota(jnp.int32, (PANEL, PANEL), 1)
     eye = jnp.where(rowi == coli, 1.0, 0.0).astype(F32)
-    upper = coli >= rowi
-    lower = coli <= rowi
     scale = 1.0 / 128.0
 
     high = hi_ref[...]
-    aug[:, :PANEL] = high
-    aug[:, PANEL:] = eye
-    eliminate(aug)
-    r_one = jnp.where(upper, aug[:, :PANEL], 0.0)
-    x_one = jnp.where(lower, aug[:, PANEL:], 0.0)
+    eliminate(high, rbuf.at[0], xbuf.at[0])
+    r_one = rbuf[0]
+    x_one = xbuf[0]
     first_ref[0] = r_one * scale
 
     l0, l1, l2, l3, l4 = gram_levels(r_one)
@@ -347,11 +396,9 @@
     d, e2 = two_sum(d, -l1)
     delta = (d - l2) + (((e1 + e2) + lo_ref[...]) - (l3 + l4))
     gram_two = eye + hdot(hdot(x_one, delta), x_one, (1, 1))
-    aug[:, :PANEL] = gram_two
-    aug[:, PANEL:] = eye
-    eliminate(aug)
-    r_two = jnp.where(upper, aug[:, :PANEL], 0.0)
-    x_two = jnp.where(lower, aug[:, PANEL:], 0.0)
+    eliminate(gram_two, rbuf.at[1], xbuf.at[1])
+    r_two = rbuf[1]
+    x_two = xbuf[1]
     r_factor = hdot(r_two, r_one)
 
     slab = slab_ref[...]
@@ -405,7 +452,7 @@
         ),
         in_specs=[VMEM_SPEC] * 7,
         out_specs=(VMEM_SPEC,) * 4,
-        scratch_shapes=[pltpu.VMEM((PANEL, 2 * PANEL), F32)],
+        scratch_shapes=[pltpu.VMEM((2, PANEL, PANEL), F32)] * 2,
         compiler_params=pltpu.CompilerParams(vmem_limit_bytes=32 * 1024 * 1024),
         name="factor",
     )(matrix_slab, pivots, panel, lead, inner, high, low)

time: 82.6 us -> 61 us (0.74)
  the two profiles are of different devices: /device:TPU:1 before, /device:TPU:8 now
where the time goes in v2:
time: 61 us; the launch traced here: 60.9 us
  Pallas kernels  56.9 us (93%)
  local copies, waits for them, and re-layouts  3.31 us (5%)
  between operations  0.65 us (1%)
    pallas_call x1, Pallas kernels, shards(): pl.pallas_call(gather_kernel, out_shape=(flat(rows, PANEL), flat(rows, PA...  43.8 us
    pallas_call x1, Pallas kernels, shards(): pl.pallas_call(factor_kernel, out_shape=(flat(1, rows, PANEL), flat(1, PA...  13.1 us
    unnamed x7, local copies, waits for them, and re-layouts  3.31 us

profile of v2, /device:TPU:8, one launch (start us, length us, event | category | flops | bytes accessed | tf_op | source)
XLA Modules:
  0.0 60.9 jit_solution(4168708059258442891)
XLA Ops:
  0.6 0.0 copy-start
  0.6 1.0 %copy-done = f32[256,512]{1,0:T(8,128)S(1)} copy-done((f32[256,512]{1,0:T(8,128)S(1)}, f32[256,512]{1,0:T(8,128)}, u32[]{:S(2)}) %copy-start) | copy-done | bytes 524312
  1.7 0.0 copy-start.1
  1.7 0.9 %copy-done.1 = f32[144,256]{1,0:T(8,128)S(1)} copy-done((f32[144,256]{1,0:T(8,128)S(1)}, f32[144,256]{1,0:T(8,128)}, u32[]{:S(2)}) %copy-start.1) | copy-done | bytes 147480
  2.6 0.0 copy-start.2
  2.6 0.7 %copy-done.2 = s32[1,128]{1,0:T(1,128)S(1)} copy-done((s32[1,128]{1,0:T(1,128)S(1)}, s32[1,128]{1,0:T(1,128)}, u32[]{:S(2)}) %copy-start.2) | copy-done | bytes 536
  3.2 43.8 %gather.1 = (f32[256,128]{1,0:T(8,128)S(1)}, f32[256,128]{1,0:T(8,128)S(1)}, f32[128,512]{1,0:T(8,128)S(1)}, f32[128,128]{1,0:T(8,128)S(1)}, f32[128,128]{1,0:T(8,128)S(1)}, /*index=5*/f32[1,144,512]{2,1,0:T(8,128)S(1)}) custom-call(f32[256,512]{1,0:T(8,128)S(1)} %copy-done, f32[144,256]{1,0:T(8,128)S(1)} %copy-done.1, s32[1,128]{1,0:T(1,128)S(1)} %copy-done.2), custom_call_target="tpu_custom_call" | custom-call | tf_op jit(solution)/shard_map/gather/pallas_call | solution.py:424
  47.1 13.1 %factor.1 = (f32[1,256,128]{2,1,0:T(8,128)}, f32[1,128,512]{2,1,0:T(8,128)}, f32[1,128,128]{2,1,0:T(8,128)}, f32[256,512]{1,0:T(8,128)}) custom-call(f32[256,512]{1,0:T(8,128)S(1)} %copy-done, s32[1,128]{1,0:T(1,128)S(1)} %copy-done.2, f32[256,128]{1,0:T(8,128)S(1)} %get-tuple-element.16.p_ref, f32[256,128]{1,0:T(8,128)S(1)} %get-tuple-element.17.lead_ref, ...), custom_call_target="tpu_custom_call" | custom-call | tf_op jit(solution)/shard_map/factor/pallas_call | solution.py:448
  60.2 0.7 %copy.9 = f32[1,144,512]{2,1,0:T(8,128)} copy(f32[1,144,512]{2,1,0:T(8,128)S(1)} %get-tuple-element.30) | data formatting | bytes 589824
Async XLA Ops:
  0.6 1.0 %copy-start = (f32[256,512]{1,0:T(8,128)S(1)}, f32[256,512]{1,0:T(8,128)}, u32[]{:S(2)}) copy-start(f32[256,512]{1,0:T(8,128)} %slab_ref.3) | copy-start | bytes 1572868
  1.7 0.9 %copy-start.1 = (f32[144,256]{1,0:T(8,128)S(1)}, f32[144,256]{1,0:T(8,128)}, u32[]{:S(2)}) copy-start(f32[144,256]{1,0:T(8,128)} %sketch_ref.1) | copy-start | bytes 442372
  2.6 0.7 %copy-start.2 = (s32[1,128]{1,0:T(1,128)S(1)}, s32[1,128]{1,0:T(1,128)}, u32[]{:S(2)}) copy-start(s32[1,128]{1,0:T(1,128)} %piv_ref.3) | copy-start | bytes 1540

commit v3 on v2

--- a/solution.py
+++ b/solution.py
@@ -86,14 +86,15 @@
     )
 
 
-def gather_kernel(
+def reduce_kernel(
+    slab_hbm, sketch_hbm, piv_hbm,
+    b_ref, p_ref, g_ref, s_ref, r_out, x_out,
     slab_ref, sketch_ref, piv_ref,
-    p_ref, lead_ref, g_ref, hi_ref, lo_ref, s_ref,
     pk, pp, rc1, rc2, leadbuf,
     wpart, wa, wsum, wb, wfull,
     gpart, ga, gsum, gb, gfull,
     spart, sa, ssum, sb, sb9, sfull,
-    sem1, sem_lead, wa_sem, wb_sem, wc_sem, ga_sem, gb_sem, gc_sem, gd_sem,
+    sem_in, sem1, sem_lead, wa_sem, wb_sem, wc_sem, ga_sem, gb_sem, gc_sem, gd_sem,
     sa_sem, sb_sem, sb9_sem, sc_sem, sd_sem,
 ):
     r = lax.axis_index("row")
@@ -101,6 +102,12 @@
     z = lax.rem(lax.div(r, 2), NZ)
     q = lax.div(r, 16) * 2 + lax.rem(r, 2)
     width = slab_ref.shape[1]
+    load_piv = pltpu.make_async_copy(piv_hbm, piv_ref, sem_in.at[0])
+    load_slab = pltpu.make_async_copy(slab_hbm, slab_ref, sem_in.at[1])
+    load_sketch = pltpu.make_async_copy(sketch_hbm, sketch_ref, sem_in.at[2])
+    load_piv.start()
+    load_slab.start()
+    load_sketch.start()
 
     def yx_row(t):
         return lax.div(t, 2) * 16 + z * 2 + lax.rem(t, 2)
@@ -121,9 +128,12 @@
             barrier, inc=1, device_id=(z_row(lax.rem(z + i, NZ)), c), device_id_type=MESH
         )
 
+    load_piv.wait()
+    onehot = pivot_onehot(piv_ref[...], c * width, width)
+    load_slab.wait()
     slab = slab_ref[...]
-    onehot = pivot_onehot(piv_ref[...], c * width, width)
     pk[...] = select_dot(slab, onehot)
+    load_sketch.wait()
     pl.semaphore_wait(barrier, NYX * NCOL - 1 + NZ - 1)
 
     core = c + 1 - 2 * lax.rem(c, 2)
@@ -201,8 +211,8 @@
         remote(leadbuf.at[0], leadbuf.at[1], sem_lead.at[0], sem_lead.at[3], (r, c)).wait_recv()
 
     lead = jnp.where(c == 0, leadbuf[0], leadbuf[1])
-    lead_ref[...] = lead
     swapped = swapped_columns(slab, lead, onehot)
+    b_ref[...] = swapped
     inner = hdot(panel, swapped, (0, 0))
     for b in range(4):
         gpart[16 * b : 16 * b + 16] = inner[:, 128 * b : 128 * b + 128].reshape(16, 8, 128)
@@ -259,6 +269,16 @@
         lambda t: sfull.at[q * 9 + z], lambda m: sfull.at[q * 9 + m], sc_sem.at[0], sc_sem.at[1]
     )
 
+    for i in range(NYX):
+        for j in range(NCOL):
+            if i or j:
+                o = lax.rem(c + j, NCOL) * 8 + lax.rem(q + i, NYX)
+                remote(wfull.at[o], wfull.at[o], wc_sem.at[0, o], wc_sem.at[1, o], (r, c)).wait_recv()
+    first_half = wfull[0:16].reshape(PANEL, PANEL)
+    second_half = wfull[16:32].reshape(PANEL, PANEL)
+    high = jnp.where(left, first_half, pltpu.roll(second_half, 64, 1))
+    low = jnp.where(left, pltpu.roll(first_half, 64, 1), second_half)
+
     arrived(z, NZ, lambda t: gb.at[t], gb_sem.at[0], gb_sem.at[1])
     total = gb[0]
     for k in range(1, NZ):
@@ -267,25 +287,28 @@
     zz(
         lambda t: gfull.at[q * 8 + z], lambda m: gfull.at[q * 8 + m], gc_sem.at[0], gc_sem.at[1]
     )
-
     arrived(z, NZ, lambda t: sfull.at[q * 9 + t], sc_sem.at[0], sc_sem.at[1])
     yx(
         lambda t: sfull.at[pl.ds(q * 9, 9)], lambda m: sfull.at[pl.ds(m * 9, 9)], sd_sem.at[0], sd_sem.at[1]
     )
+
+    eliminate(high, r_out.at[0], x_out.at[0])
+    r_one = r_out[0]
+    x_one = x_out[0]
+
     arrived(z, NZ, lambda t: gfull.at[q * 8 + t], gc_sem.at[0], gc_sem.at[1])
     yx(
         lambda t: gfull.at[pl.ds(q * 8, 8)], lambda m: gfull.at[pl.ds(m * 8, 8)], gd_sem.at[0], gd_sem.at[1]
     )
 
-    for i in range(NYX):
-        for j in range(NCOL):
-            if i or j:
-                o = lax.rem(c + j, NCOL) * 8 + lax.rem(q + i, NYX)
-                remote(wfull.at[o], wfull.at[o], wc_sem.at[0, o], wc_sem.at[1, o], (r, c)).wait_recv()
-    first_half = wfull[0:16].reshape(PANEL, PANEL)
-    second_half = wfull[16:32].reshape(PANEL, PANEL)
-    hi_ref[...] = jnp.where(left, first_half, pltpu.roll(second_half, 64, 1))
-    lo_ref[...] = jnp.where(left, pltpu.roll(first_half, 64, 1), second_half)
+    rowi = lax.broadcasted_iota(jnp.int32, (PANEL, PANEL), 0)
+    eye = jnp.where(rowi == lane, 1.0, 0.0).astype(F32)
+    l0, l1, l2, l3, l4 = gram_levels(r_one)
+    d, e1 = two_sum(high, -l0)
+    d, e2 = two_sum(d, -l1)
+    delta = (d - l2) + (((e1 + e2) + low) - (l3 + l4))
+    gram_two = eye + hdot(hdot(x_one, delta), x_one, (1, 1))
+    eliminate(gram_two, r_out.at[1], x_out.at[1])
 
     arrived(q, NYX, lambda t: sfull.at[pl.ds(t * 9, 9)], sd_sem.at[0], sd_sem.at[1])
     for b in range(4):
@@ -374,89 +397,91 @@
                 blocks[k] = jnp.where(inside, 0.0, blocks[k]) - update[8 * k : 8 * k + 8, :]
 
 
-def factor_kernel(
-    slab_ref, piv_ref, p_ref, lead_ref, g_ref, hi_ref, lo_ref,
-    q_ref, r_ref, first_ref, out_ref, rbuf, xbuf,
+def update_kernel(
+    b_ref, p_ref, g_ref, s_in, r_ref, x_ref,
+    s_hbm, q_hbm, e_hbm, first_hbm, out_hbm,
+    qbuf, ebuf, fbuf, obuf, sem,
 ):
-    c = lax.axis_index("col")
-    width = slab_ref.shape[1]
-    rowi = lax.broadcasted_iota(jnp.int32, (PANEL, PANEL), 0)
-    coli = lax.broadcasted_iota(jnp.int32, (PANEL, PANEL), 1)
-    eye = jnp.where(rowi == coli, 1.0, 0.0).astype(F32)
+    lead_block = lax.axis_index("col") == 0
+    copies = [pltpu.make_async_copy(s_in, s_hbm, sem.at[0])]
+    copies[0].start()
     scale = 1.0 / 128.0
 
-    high = hi_ref[...]
-    eliminate(high, rbuf.at[0], xbuf.at[0])
-    r_one = rbuf[0]
-    x_one = xbuf[0]
-    first_ref[0] = r_one * scale
-
-    l0, l1, l2, l3, l4 = gram_levels(r_one)
-    d, e1 = two_sum(high, -l0)
-    d, e2 = two_sum(d, -l1)
-    delta = (d - l2) + (((e1 + e2) + lo_ref[...]) - (l3 + l4))
-    gram_two = eye + hdot(hdot(x_one, delta), x_one, (1, 1))
-    eliminate(gram_two, rbuf.at[1], xbuf.at[1])
-    r_two = rbuf[1]
-    x_two = xbuf[1]
-    r_factor = hdot(r_two, r_one)
-
-    slab = slab_ref[...]
-    onehot = pivot_onehot(piv_ref[...], c * width, width)
-    swapped = swapped_columns(slab, lead_ref[...], onehot)
-    basis = hdot(hdot(p_ref[...], x_one, (1, 1)), x_two, (1, 1))
-    projected = hdot(x_two, hdot(x_one, g_ref[...]))
-    q_ref[0] = basis * 128.0
-    lead_block = c == 0
-    r_ref[0, :, :PANEL] = jnp.where(lead_block, r_factor, projected[:, :PANEL]) * scale
-    r_ref[0, :, PANEL:] = projected[:, PANEL:] * scale
-    rest = swapped - hdot(basis, projected)
-    out_ref[:, :PANEL] = jnp.where(lead_block, 0.0, rest[:, :PANEL])
-    out_ref[:, PANEL:] = rest[:, PANEL:]
+    def store(k, src, dst):
+        copy = pltpu.make_async_copy(src, dst, sem.at[k])
+        copy.start()
+        copies.append(copy)
+
+    r_one = r_ref[0]
+    fbuf[...] = r_one * scale
+    store(1, fbuf, first_hbm.at[0])
+    inverse = hdot(x_ref[1], x_ref[0])
+    basis = hdot(p_ref[...], inverse, (1, 1))
+    qbuf[...] = basis * 128.0
+    store(2, qbuf, q_hbm.at[0])
+    r_factor = hdot(r_ref[1], r_one)
+    for k in range(4):
+        cols = slice(128 * k, 128 * k + 128)
+        projected = hdot(inverse, g_ref[:, cols])
+        rest = b_ref[:, cols] - hdot(basis, projected)
+        if k == 0:
+            projected = jnp.where(lead_block, r_factor, projected)
+            rest = jnp.where(lead_block, 0.0, rest)
+        ebuf[:, cols] = projected * scale
+        obuf[:, cols] = rest
+        store(3 + k, obuf.at[:, cols], out_hbm.at[:, cols])
+    store(7, ebuf, e_hbm.at[0])
+    for copy in copies:
+        copy.wait()
 
 
 def shards(matrix_slab, sketch_matrix, pivots):
     rows, width = matrix_slab.shape
     sk = sketch_matrix.shape[0]
     dma = pltpu.SemaphoreType.DMA
+    hbm = pl.BlockSpec(memory_space=pltpu.HBM)
     tile = lambda *lead: pltpu.VMEM(lead + (8, 128), F32)
     flat = lambda *shape: jax.ShapeDtypeStruct(shape, F32)
-    panel, lead, inner, high, low, sketches = pl.pallas_call(
-        gather_kernel,
+    swapped, panel, inner, sketches, factors, inverses = pl.pallas_call(
+        reduce_kernel,
         out_shape=(
-            flat(rows, PANEL), flat(rows, PANEL), flat(PANEL, width),
-            flat(PANEL, PANEL), flat(PANEL, PANEL), flat(1, sk, width),
+            flat(rows, width), flat(rows, PANEL), flat(PANEL, width), flat(1, sk, width),
+            flat(2, PANEL, PANEL), flat(2, PANEL, PANEL),
         ),
-        in_specs=[VMEM_SPEC] * 3,
+        in_specs=[hbm] * 3,
         out_specs=(VMEM_SPEC,) * 6,
         scratch_shapes=[
+            pltpu.VMEM((rows, width), F32), pltpu.VMEM((sk, rows), F32), pltpu.VMEM((1, PANEL), jnp.int32),
             pltpu.VMEM((rows, PANEL), F32), pltpu.VMEM((rows, PANEL), F32),
             pltpu.VMEM((rows, PANEL), F32), pltpu.VMEM((rows, PANEL), F32),
             pltpu.VMEM((2, rows, PANEL), F32),
             tile(32), tile(8), tile(2), tile(8), tile(32),
             tile(64), tile(8, 8), tile(8), tile(8), tile(64),
             tile(72), tile(8, 9), tile(9), tile(8), tile(8), tile(72),
-            dma((4,)), dma((4,)), dma((2, 8)), dma((2, 8)), dma((2, 32)),
+            dma((3,)), dma((4,)), dma((4,)), dma((2, 8)), dma((2, 8)), dma((2, 32)),
             dma((2, 8)), dma((2, 8)), dma((2, 8)), dma((2, 8)),
             dma((2, 8)), dma((2, 8)), dma((2, 8)), dma((2, 8)), dma((2, 8)),
         ],
         compiler_params=pltpu.CompilerParams(
             collective_id=0, has_side_effects=True, vmem_limit_bytes=32 * 1024 * 1024
         ),
-        name="gather",
+        name="reduce",
     )(matrix_slab, sketch_matrix, pivots)
-    q_panels, r_factors, first, slab_out = pl.pallas_call(
-        factor_kernel,
+    return pl.pallas_call(
+        update_kernel,
         out_shape=(
-            flat(1, rows, PANEL), flat(1, PANEL, width), flat(1, PANEL, PANEL), flat(rows, width),
+            flat(1, sk, width), flat(1, rows, PANEL), flat(1, PANEL, width),
+            flat(1, PANEL, PANEL), flat(rows, width),
         ),
-        in_specs=[VMEM_SPEC] * 7,
-        out_specs=(VMEM_SPEC,) * 4,
-        scratch_shapes=[pltpu.VMEM((2, PANEL, PANEL), F32)] * 2,
+        in_specs=[VMEM_SPEC] * 3 + [pl.BlockSpec(memory_space=pl.ANY)] + [VMEM_SPEC] * 2,
+        out_specs=(hbm,) * 5,
+        scratch_shapes=[
+            pltpu.VMEM((rows, PANEL), F32), pltpu.VMEM((PANEL, width), F32),
+            pltpu.VMEM((PANEL, PANEL), F32), pltpu.VMEM((rows, width), F32), dma((8,)),
+        ],
         compiler_params=pltpu.CompilerParams(vmem_limit_bytes=32 * 1024 * 1024),
-        name="factor",
-    )(matrix_slab, pivots, panel, lead, inner, high, low)
-    return sketches, q_panels, r_factors, first, slab_out
+        name="update",
+    )(swapped, panel, inner, sketches, factors, inverses)
 
 
 def solution(mesh):

time: 61 us -> 52.4 us (0.86)
  the two profiles are of different devices: /device:TPU:8 before, /device:TPU:1 now
where the time goes in v3:
time: 52.4 us; the launch traced here: 52.2 us
  Pallas kernels  49 us (94%)
  local copies, waits for them, and re-layouts  2.6 us (5%)
  between operations  0.65 us (1%)
    pallas_call x1, Pallas kernels, shards(): pl.pallas_call(reduce_kernel, out_shape=(flat(rows, width), flat(rows, PA...  46.7 us
    unnamed x6, local copies, waits for them, and re-layouts  2.6 us
    pallas_call x1, Pallas kernels, shards(): pl.pallas_call(update_kernel, out_shape=(flat(1, sk, width), flat(1, rows...  2.24 us

profile of v3, /device:TPU:1, one launch (start us, length us, event | category | flops | bytes accessed | tf_op | source)
XLA Modules:
  0.0 52.2 jit_solution(13634358581957558104)
XLA Ops:
  0.6 0.0 copy-start
  0.6 1.0 %copy-done = f32[256,512]{1,0:T(8,128)S(1)} copy-done((f32[256,512]{1,0:T(8,128)S(1)}, f32[256,512]{1,0:T(8,128)}, u32[]{:S(2)}) %copy-start) | copy-done | bytes 524312
  1.7 0.0 copy-start.1
  1.7 0.9 %copy-done.1 = f32[144,256]{1,0:T(8,128)S(1)} copy-done((f32[144,256]{1,0:T(8,128)S(1)}, f32[144,256]{1,0:T(8,128)}, u32[]{:S(2)}) %copy-start.1) | copy-done | bytes 147480
  2.6 0.0 copy-start.2
  2.6 0.7 %copy-done.2 = s32[1,128]{1,0:T(1,128)S(1)} copy-done((s32[1,128]{1,0:T(1,128)S(1)}, s32[1,128]{1,0:T(1,128)}, u32[]{:S(2)}) %copy-start.2) | copy-done | bytes 536
  3.2 46.7 %reduce.1 = (f32[256,512]{1,0:T(8,128)S(1)}, f32[256,128]{1,0:T(8,128)S(1)}, f32[128,512]{1,0:T(8,128)S(1)}, f32[1,144,512]{2,1,0:T(8,128)S(1)}, f32[2,128,128]{2,1,0:T(8,128)S(1)}, /*index=5*/f32[2,128,128]{2,1,0:T(8,128)S(1)}) custom-call(f32[256,512]{1,0:T(8,128)S(1)} %copy-done, f32[144,256]{1,0:T(8,128)S(1)} %copy-done.1, s32[1,128]{1,0:T(1,128)S(1)} %copy-done.2), custom_call_target="tpu_custom_call" | custom-call | tf_op jit(solution)/shard_map/reduce/pallas_call | solution.py:445
  50.0 2.2 %update.1 = (f32[1,144,512]{2,1,0:T(8,128)}, f32[1,256,128]{2,1,0:T(8,128)}, f32[1,128,512]{2,1,0:T(8,128)}, f32[1,128,128]{2,1,0:T(8,128)}, f32[256,512]{1,0:T(8,128)}) custom-call(f32[256,512]{1,0:T(8,128)S(1)} %get-tuple-element.11.b_ref, f32[256,128]{1,0:T(8,128)S(1)} %get-tuple-element.12.p_ref, f32[128,512]{1,0:T(8,128)S(1)} %get-tuple-element.13.g_ref, ...), custom_call_target="tpu_custom_call" | custom-call | tf_op jit(solution)/shard_map/update/pallas_call | solution.py:470
Async XLA Ops:
  0.6 1.0 %copy-start = (f32[256,512]{1,0:T(8,128)S(1)}, f32[256,512]{1,0:T(8,128)}, u32[]{:S(2)}) copy-start(f32[256,512]{1,0:T(8,128)} %slab_hbm.1) | copy-start | bytes 1572868
  1.7 0.9 %copy-start.1 = (f32[144,256]{1,0:T(8,128)S(1)}, f32[144,256]{1,0:T(8,128)}, u32[]{:S(2)}) copy-start(f32[144,256]{1,0:T(8,128)} %sketch_hbm.1) | copy-start | bytes 442372
  2.6 0.7 %copy-start.2 = (s32[1,128]{1,0:T(1,128)S(1)}, s32[1,128]{1,0:T(1,128)}, u32[]{:S(2)}) copy-start(s32[1,128]{1,0:T(1,128)} %piv_hbm.1) | copy-start | bytes 1540

commit v4 on v3

--- a/solution.py
+++ b/solution.py
@@ -9,8 +9,8 @@
 from jax.sharding import PartitionSpec as P
 
 PANEL = 128
-NYX = 8
-NZ = 8
+NY = 4
+NZX = 16
 NCOL = 4
 MESH = pl.DeviceIdType.MESH
 F32 = jnp.float32
@@ -91,16 +91,16 @@
     b_ref, p_ref, g_ref, s_ref, r_out, x_out,
     slab_ref, sketch_ref, piv_ref,
     pk, pp, rc1, rc2, leadbuf,
-    wpart, wa, wsum, wb, wfull,
+    wpart, wa, wsum, wb, wtot, wfull,
     gpart, ga, gsum, gb, gfull,
-    spart, sa, ssum, sb, sb9, sfull,
+    spart, sa, ssum, sb, sbx, sfull,
     sem_in, sem1, sem_lead, wa_sem, wb_sem, wc_sem, ga_sem, gb_sem, gc_sem, gd_sem,
-    sa_sem, sb_sem, sb9_sem, sc_sem, sd_sem,
+    sa_sem, sb_sem, sbx_sem, sc_sem, sd_sem,
 ):
     r = lax.axis_index("row")
     c = lax.axis_index("col")
-    z = lax.rem(lax.div(r, 2), NZ)
-    q = lax.div(r, 16) * 2 + lax.rem(r, 2)
+    y = lax.div(r, NZX)
+    w = lax.rem(r, NZX)
     width = slab_ref.shape[1]
     load_piv = pltpu.make_async_copy(piv_hbm, piv_ref, sem_in.at[0])
     load_slab = pltpu.make_async_copy(slab_hbm, slab_ref, sem_in.at[1])
@@ -109,24 +109,17 @@
     load_slab.start()
     load_sketch.start()
 
-    def yx_row(t):
-        return lax.div(t, 2) * 16 + z * 2 + lax.rem(t, 2)
-
-    def z_row(t):
-        return lax.div(r, 16) * 16 + t * 2 + lax.rem(r, 2)
+    y_peers = [(lax.rem(y + i, NY), i) for i in range(1, NY)]
+    zx_peers = [lax.rem(w + i, NZX) for i in range(1, NZX)]
+    yc_peers = [
+        (lax.rem(y + i, NY), lax.rem(c + j, NCOL)) for i in range(NY) for j in range(NCOL) if i or j
+    ]
 
     barrier = pltpu.get_barrier_semaphore()
-    for i in range(NYX):
-        for j in range(NCOL):
-            if i or j:
-                pl.semaphore_signal(
-                    barrier, inc=1, device_id_type=MESH,
-                    device_id=(yx_row(lax.rem(q + i, NYX)), lax.rem(c + j, NCOL)),
-                )
-    for i in range(1, NZ):
-        pl.semaphore_signal(
-            barrier, inc=1, device_id=(z_row(lax.rem(z + i, NZ)), c), device_id_type=MESH
-        )
+    for t in zx_peers:
+        pl.semaphore_signal(barrier, inc=1, device_id=(y * NZX + t, c), device_id_type=MESH)
+    for t, d in yc_peers:
+        pl.semaphore_signal(barrier, inc=1, device_id=(t * NZX + w, d), device_id_type=MESH)
 
     load_piv.wait()
     onehot = pivot_onehot(piv_ref[...], c * width, width)
@@ -134,24 +127,60 @@
     slab = slab_ref[...]
     pk[...] = select_dot(slab, onehot)
     load_sketch.wait()
-    pl.semaphore_wait(barrier, NYX * NCOL - 1 + NZ - 1)
+    sketch = hdot(sketch_ref[...], slab)
+    for b in range(4):
+        spart[b] = sketch[:, 128 * b : 128 * b + 128]
+    leadbuf[0] = slab[:, :PANEL]
+    pl.semaphore_wait(barrier, NZX - 1 + NY * NCOL - 1)
+
+    pending = []
+
+    def send(src, dst, send_sem, recv_sem, device):
+        copy = remote(src, dst, send_sem, recv_sem, device)
+        copy.start()
+        pending.append(copy)
+
+    def to_y(src, dst, sems):
+        for t, _ in y_peers:
+            send(src(t), dst(y), sems.at[0, t], sems.at[1, y], (t * NZX + w, c))
+
+    def to_zx(src, dst, sems):
+        for t in zx_peers:
+            send(src(t), dst(w), sems.at[0, t], sems.at[1, w], (y * NZX + t, c))
+
+    def from_y(dst, sems):
+        for t, _ in y_peers:
+            remote(dst(t), dst(t), sems.at[0, t], sems.at[1, t], (r, c)).wait_recv()
+
+    def from_zx(dst, sems):
+        for t in zx_peers:
+            remote(dst(t), dst(t), sems.at[0, t], sems.at[1, t], (r, c)).wait_recv()
+
+    def total_of(buf, count):
+        return tree_sum([buf[k] for k in range(count)])
+
+    def two_float_total(buf, count):
+        total = buf[0]
+        err = jnp.zeros_like(total)
+        for k in range(1, count):
+            total, e = two_sum(total, buf[k])
+            err = err + e
+        lane16 = lax.broadcasted_iota(jnp.int32, total.shape, 1)
+        return jnp.where(lane16 < 64, total, total + pltpu.roll(err, 64, 1))
 
     core = c + 1 - 2 * lax.rem(c, 2)
     chip = lax.rem(c + 2, NCOL)
     first = remote(pk, rc1, sem1.at[0], sem1.at[1], (r, core))
     first.start()
-    sketch = hdot(sketch_ref[...], slab)
-    for b in range(4):
-        spart[18 * b : 18 * b + 18] = sketch[:, 128 * b : 128 * b + 128].reshape(18, 8, 128)
+    to_y(lambda t: spart.at[t], lambda m: sa.at[m], sa_sem)
+    sa[y] = spart[y]
     first.wait_recv()
     pp[...] = pk[...] + rc1[...]
     second = remote(pp, rc2, sem1.at[2], sem1.at[3], (r, chip))
     second.start()
-
     lead_copies = [
         remote(leadbuf.at[0], leadbuf.at[1], sem_lead.at[j - 1], sem_lead.at[3], (r, j)) for j in range(1, NCOL)
     ]
-    leadbuf[0] = slab[:, :PANEL]
 
     @pl.when(c == 0)
     def _():
@@ -159,52 +188,27 @@
             copy.start()
 
     second.wait_recv()
+    pending.extend([first, second])
     panel = pp[...] + rc2[...]
-    p_ref[...] = panel
 
     lane = lax.broadcasted_iota(jnp.int32, (PANEL, PANEL), 1)
+    left = lane < 64
     l0, l1, l2, l3, l4 = gram_levels(panel)
     high, low = two_sum(l0, l1)
     high, low2 = two_sum(high, l2)
     low = (low + low2) + (l3 + l4)
-    left = lane < 64
-    wpart[0:16] = jnp.where(left, high, pltpu.roll(low, 64, 1)).reshape(16, 8, 128)
-    wpart[16:32] = jnp.where(left, pltpu.roll(high, 64, 1), low).reshape(16, 8, 128)
-
-    pending = [first, second]
-
-    def exchange(me, count, row_of, src, dst, send_sems, recv_sems):
-        copies = []
-        for i in range(1, count):
-            t = lax.rem(me + i, count)
-            copy = remote(src(t), dst(me), send_sems.at[t], recv_sems.at[me], (row_of(t), c))
-            copy.start()
-            copies.append(copy)
-        pending.extend(copies)
-
-    def arrived(me, count, dst, send_sems, recv_sems):
-        for i in range(1, count):
-            t = lax.rem(me + i, count)
-            remote(dst(t), dst(t), send_sems.at[t], recv_sems.at[t], (r, c)).wait_recv()
-
-    yx = functools.partial(exchange, q, NYX, yx_row)
-    zz = functools.partial(exchange, z, NZ, z_row)
-
-    def two_float_total(buf):
-        total = buf[0]
-        err = jnp.zeros((8, 128), F32)
-        for k in range(1, 8):
-            total, e = two_sum(total, buf[k])
-            err = err + e
-        lane8 = lax.broadcasted_iota(jnp.int32, (8, 128), 1)
-        return jnp.where(lane8 < 64, total, total + pltpu.roll(err, 64, 1))
-
-    yx(lambda t: wpart.at[c * 8 + t], lambda m: wa.at[m], wa_sem.at[0], wa_sem.at[1])
-    yx(
-        lambda t: spart.at[pl.ds(9 * t, 9)], lambda m: sa.at[m], sa_sem.at[0], sa_sem.at[1]
-    )
-    wa[q] = wpart[c * 8 + q]
-    sa[q] = spart[pl.ds(9 * q, 9)]
+    wpart[0:8] = jnp.where(left, high, pltpu.roll(low, 64, 1)).reshape(8, 16, 128)
+    wpart[8:16] = jnp.where(left, pltpu.roll(high, 64, 1), low).reshape(8, 16, 128)
+    to_y(lambda t: wpart.at[c * 4 + t], lambda m: wa.at[m], wa_sem)
+    wa[y] = wpart[c * 4 + y]
+    p_ref[...] = panel
+
+    from_y(lambda t: sa.at[t], sa_sem)
+    ssum[...] = total_of(sa, NY)
+    to_zx(lambda t: ssum.at[pl.ds(8 * t, 8)], lambda m: sb.at[m], sb_sem)
+    to_zx(lambda t: ssum.at[pl.ds(128, 16)], lambda m: sbx.at[m], sbx_sem)
+    sb[w] = ssum[pl.ds(pl.multiple_of(8 * w, 8), 8)]
+    sbx[w] = ssum[pl.ds(128, 16)]
 
     @pl.when(c != 0)
     def _():
@@ -215,91 +219,55 @@
     b_ref[...] = swapped
     inner = hdot(panel, swapped, (0, 0))
     for b in range(4):
-        gpart[16 * b : 16 * b + 16] = inner[:, 128 * b : 128 * b + 128].reshape(16, 8, 128)
-
-    arrived(q, NYX, lambda t: wa.at[t], wa_sem.at[0], wa_sem.at[1])
-    wsum[0] = two_float_total(wa)
-    zz(lambda t: wsum.at[0], lambda m: wb.at[m], wb_sem.at[0], wb_sem.at[1])
-    yx(lambda t: gpart.at[pl.ds(8 * t, 8)], lambda m: ga.at[m], ga_sem.at[0], ga_sem.at[1])
-    wb[z] = wsum[0]
-    ga[q] = gpart[pl.ds(8 * q, 8)]
-
-    arrived(q, NYX, lambda t: sa.at[t], sa_sem.at[0], sa_sem.at[1])
-    total = sa[0]
-    for k in range(1, NYX):
-        total = total + sa[k]
-    ssum[...] = total
-    zz(lambda t: ssum.at[t], lambda m: sb.at[m], sb_sem.at[0], sb_sem.at[1])
-    zz(lambda t: ssum.at[8], lambda m: sb9.at[m], sb9_sem.at[0], sb9_sem.at[1])
-    sb[z] = ssum[z]
-    sb9[z] = ssum[8]
-
-    arrived(z, NZ, lambda t: wb.at[t], wb_sem.at[0], wb_sem.at[1])
-    mine = c * 8 + q
-    wsum[1] = two_float_total(wb)
-    for i in range(NYX):
-        for j in range(NCOL):
-            if i or j:
-                t = lax.rem(q + i, NYX)
-                d = lax.rem(c + j, NCOL)
-                copy = remote(
-                    wsum.at[1], wfull.at[mine], wc_sem.at[0, d * 8 + t], wc_sem.at[1, mine], (yx_row(t), d)
-                )
-                copy.start()
-                pending.append(copy)
-    wfull[mine] = wsum[1]
-
-    arrived(q, NYX, lambda t: ga.at[t], ga_sem.at[0], ga_sem.at[1])
-    total = ga[0]
-    for k in range(1, NYX):
-        total = total + ga[k]
-    gsum[...] = total
-    zz(lambda t: gsum.at[t], lambda m: gb.at[m], gb_sem.at[0], gb_sem.at[1])
-    gb[z] = gsum[z]
-
-    arrived(z, NZ, lambda t: sb.at[t], sb_sem.at[0], sb_sem.at[1])
-    arrived(z, NZ, lambda t: sb9.at[t], sb9_sem.at[0], sb9_sem.at[1])
-    total, ninth = sb[0], sb9[0]
-    for k in range(1, NZ):
-        total = total + sb[k]
-        ninth = ninth + sb9[k]
-    sfull[q * 9 + z] = total
-    sfull[q * 9 + 8] = ninth
-    zz(
-        lambda t: sfull.at[q * 9 + z], lambda m: sfull.at[q * 9 + m], sc_sem.at[0], sc_sem.at[1]
-    )
-
-    for i in range(NYX):
-        for j in range(NCOL):
-            if i or j:
-                o = lax.rem(c + j, NCOL) * 8 + lax.rem(q + i, NYX)
-                remote(wfull.at[o], wfull.at[o], wc_sem.at[0, o], wc_sem.at[1, o], (r, c)).wait_recv()
-    first_half = wfull[0:16].reshape(PANEL, PANEL)
-    second_half = wfull[16:32].reshape(PANEL, PANEL)
+        gpart[b] = inner[:, 128 * b : 128 * b + 128]
+    to_y(lambda t: gpart.at[t], lambda m: ga.at[m], ga_sem)
+    ga[y] = gpart[y]
+
+    from_y(lambda t: wa.at[t], wa_sem)
+    wsum[...] = two_float_total(wa, NY)
+    to_zx(lambda t: wsum, lambda m: wb.at[m], wb_sem)
+    wb[w] = wsum[...]
+
+    from_zx(lambda t: sb.at[t], sb_sem)
+    from_zx(lambda t: sbx.at[t], sbx_sem)
+    tile = lambda t: pl.ds(pl.multiple_of(8 * t, 8), 8)
+    sfull[y, tile(w)] = total_of(sb, NZX)
+    sfull[y, pl.ds(128, 16)] = total_of(sbx, NZX)
+    to_zx(lambda t: sfull.at[y, tile(w)], lambda m: sfull.at[y, tile(m)], sc_sem)
+
+    from_y(lambda t: ga.at[t], ga_sem)
+    gsum[...] = total_of(ga, NY)
+    to_zx(lambda t: gsum.at[tile(t)], lambda m: gb.at[m], gb_sem)
+    gb[w] = gsum[tile(w)]
+
+    from_zx(lambda t: wb.at[t], wb_sem)
+    wtot[...] = two_float_total(wb, NZX)
+    mine = c * 4 + y
+    for t, d in yc_peers:
+        send(wtot, wfull.at[mine], wc_sem.at[0, d * 4 + t], wc_sem.at[1, mine], (t * NZX + w, d))
+    wfull[mine] = wtot[...]
+
+    from_zx(lambda t: sfull.at[y, tile(t)], sc_sem)
+    to_y(lambda t: sfull.at[y], lambda m: sfull.at[m], sd_sem)
+
+    from_zx(lambda t: gb.at[t], gb_sem)
+    gfull[y, tile(w)] = total_of(gb, NZX)
+    to_zx(lambda t: gfull.at[y, tile(w)], lambda m: gfull.at[y, tile(m)], gc_sem)
+
+    for t, d in yc_peers:
+        o = d * 4 + t
+        remote(wfull.at[o], wfull.at[o], wc_sem.at[0, o], wc_sem.at[1, o], (r, c)).wait_recv()
+    first_half = wfull[0:8].reshape(PANEL, PANEL)
+    second_half = wfull[8:16].reshape(PANEL, PANEL)
     high = jnp.where(left, first_half, pltpu.roll(second_half, 64, 1))
     low = jnp.where(left, pltpu.roll(first_half, 64, 1), second_half)
-
-    arrived(z, NZ, lambda t: gb.at[t], gb_sem.at[0], gb_sem.at[1])
-    total = gb[0]
-    for k in range(1, NZ):
-        total = total + gb[k]
-    gfull[q * 8 + z] = total
-    zz(
-        lambda t: gfull.at[q * 8 + z], lambda m: gfull.at[q * 8 + m], gc_sem.at[0], gc_sem.at[1]
-    )
-    arrived(z, NZ, lambda t: sfull.at[q * 9 + t], sc_sem.at[0], sc_sem.at[1])
-    yx(
-        lambda t: sfull.at[pl.ds(q * 9, 9)], lambda m: sfull.at[pl.ds(m * 9, 9)], sd_sem.at[0], sd_sem.at[1]
-    )
 
     eliminate(high, r_out.at[0], x_out.at[0])
     r_one = r_out[0]
     x_one = x_out[0]
 
-    arrived(z, NZ, lambda t: gfull.at[q * 8 + t], gc_sem.at[0], gc_sem.at[1])
-    yx(
-        lambda t: gfull.at[pl.ds(q * 8, 8)], lambda m: gfull.at[pl.ds(m * 8, 8)], gd_sem.at[0], gd_sem.at[1]
-    )
+    from_zx(lambda t: gfull.at[y, tile(t)], gc_sem)
+    to_y(lambda t: gfull.at[y], lambda m: gfull.at[m], gd_sem)
 
     rowi = lax.broadcasted_iota(jnp.int32, (PANEL, PANEL), 0)
     eye = jnp.where(rowi == lane, 1.0, 0.0).astype(F32)
@@ -308,14 +276,14 @@
     d, e2 = two_sum(d, -l1)
     delta = (d - l2) + (((e1 + e2) + low) - (l3 + l4))
     gram_two = eye + hdot(hdot(x_one, delta), x_one, (1, 1))
+    from_y(lambda t: sfull.at[t], sd_sem)
+    for b in range(4):
+        s_ref[0, :, 128 * b : 128 * b + 128] = sfull[b]
     eliminate(gram_two, r_out.at[1], x_out.at[1])
 
-    arrived(q, NYX, lambda t: sfull.at[pl.ds(t * 9, 9)], sd_sem.at[0], sd_sem.at[1])
+    from_y(lambda t: gfull.at[t], gd_sem)
     for b in range(4):
-        s_ref[0, :, 128 * b : 128 * b + 128] = sfull[18 * b : 18 * b + 18].reshape(144, 128)
-    arrived(q, NYX, lambda t: gfull.at[pl.ds(t * 8, 8)], gd_sem.at[0], gd_sem.at[1])
-    for b in range(4):
-        g_ref[:, 128 * b : 128 * b + 128] = gfull[16 * b : 16 * b + 16].reshape(128, 128)
+        g_ref[:, 128 * b : 128 * b + 128] = gfull[b]
 
     for copy in pending:
         copy.wait_send()
@@ -441,6 +409,9 @@
     dma = pltpu.SemaphoreType.DMA
     hbm = pl.BlockSpec(memory_space=pltpu.HBM)
     tile = lambda *lead: pltpu.VMEM(lead + (8, 128), F32)
+    block = lambda *lead: pltpu.VMEM(lead + (16, 128), F32)
+    square = lambda *lead: pltpu.VMEM(lead + (PANEL, 128), F32)
+    tall = lambda *lead: pltpu.VMEM(lead + (sk, 128), F32)
     flat = lambda *shape: jax.ShapeDtypeStruct(shape, F32)
     swapped, panel, inner, sketches, factors, inverses = pl.pallas_call(
         reduce_kernel,
@@ -455,12 +426,12 @@
             pltpu.VMEM((rows, PANEL), F32), pltpu.VMEM((rows, PANEL), F32),
             pltpu.VMEM((rows, PANEL), F32), pltpu.VMEM((rows, PANEL), F32),
             pltpu.VMEM((2, rows, PANEL), F32),
-            tile(32), tile(8), tile(2), tile(8), tile(32),
-            tile(64), tile(8, 8), tile(8), tile(8), tile(64),
-            tile(72), tile(8, 9), tile(9), tile(8), tile(8), tile(72),
-            dma((3,)), dma((4,)), dma((4,)), dma((2, 8)), dma((2, 8)), dma((2, 32)),
-            dma((2, 8)), dma((2, 8)), dma((2, 8)), dma((2, 8)),
-            dma((2, 8)), dma((2, 8)), dma((2, 8)), dma((2, 8)), dma((2, 8)),
+            block(16), block(NY), block(), block(NZX), block(), block(16),
+            square(NY), square(NY), square(), tile(NZX), square(NY),
+            tall(NY), tall(NY), tall(), tile(NZX), block(NZX), tall(NY),
+            dma((3,)), dma((4,)), dma((4,)), dma((2, NY)), dma((2, NZX)), dma((2, 16)),
+            dma((2, NY)), dma((2, NZX)), dma((2, NZX)), dma((2, NY)),
+            dma((2, NY)), dma((2, NZX)), dma((2, NZX)), dma((2, NZX)), dma((2, NY)),
         ],
         compiler_params=pltpu.CompilerParams(
             collective_id=0, has_side_effects=True, vmem_limit_bytes=32 * 1024 * 1024

time: 52.4 us -> 52.5 us (level)
  no operation moved by 1% of the time
where the time goes in v4:
time: 52.5 us; the launch traced here: 51.8 us
  Pallas kernels  48.6 us (93%)
  local copies, waits for them, and re-layouts  2.6 us (5%)
  between operations  0.65 us (1%)
    pallas_call x1, Pallas kernels, shards(): pl.pallas_call(reduce_kernel, out_shape=(flat(rows, width), flat(rows, PA...  46.3 us
    unnamed x6, local copies, waits for them, and re-layouts  2.6 us
    pallas_call x1, Pallas kernels, shards(): pl.pallas_call(update_kernel, out_shape=(flat(1, sk, width), flat(1, rows...  2.25 us

profile of v4, /device:TPU:1, one launch (start us, length us, event | category | flops | bytes accessed | tf_op | source)
XLA Modules:
  0.0 51.8 jit_solution(8303937678199073265)
XLA Ops:
  0.6 0.0 copy-start
  0.6 1.0 %copy-done = f32[256,512]{1,0:T(8,128)S(1)} copy-done((f32[256,512]{1,0:T(8,128)S(1)}, f32[256,512]{1,0:T(8,128)}, u32[]{:S(2)}) %copy-start) | copy-done | bytes 524312
  1.7 0.0 copy-start.1
  1.7 0.9 %copy-done.1 = f32[144,256]{1,0:T(8,128)S(1)} copy-done((f32[144,256]{1,0:T(8,128)S(1)}, f32[144,256]{1,0:T(8,128)}, u32[]{:S(2)}) %copy-start.1) | copy-done | bytes 147480
  2.6 0.0 copy-start.2
  2.6 0.7 %copy-done.2 = s32[1,128]{1,0:T(1,128)S(1)} copy-done((s32[1,128]{1,0:T(1,128)S(1)}, s32[1,128]{1,0:T(1,128)}, u32[]{:S(2)}) %copy-start.2) | copy-done | bytes 536
  3.2 46.3 %reduce.1 = (f32[256,512]{1,0:T(8,128)S(1)}, f32[256,128]{1,0:T(8,128)S(1)}, f32[128,512]{1,0:T(8,128)S(1)}, f32[1,144,512]{2,1,0:T(8,128)S(1)}, f32[2,128,128]{2,1,0:T(8,128)S(1)}, /*index=5*/f32[2,128,128]{2,1,0:T(8,128)S(1)}) custom-call(f32[256,512]{1,0:T(8,128)S(1)} %copy-done, f32[144,256]{1,0:T(8,128)S(1)} %copy-done.1, s32[1,128]{1,0:T(1,128)S(1)} %copy-done.2), custom_call_target="tpu_custom_call" | custom-call | tf_op jit(solution)/shard_map/reduce/pallas_call | solution.py:416
  49.6 2.2 %update.1 = (f32[1,144,512]{2,1,0:T(8,128)}, f32[1,256,128]{2,1,0:T(8,128)}, f32[1,128,512]{2,1,0:T(8,128)}, f32[1,128,128]{2,1,0:T(8,128)}, f32[256,512]{1,0:T(8,128)}) custom-call(f32[256,512]{1,0:T(8,128)S(1)} %get-tuple-element.11.b_ref, f32[256,128]{1,0:T(8,128)S(1)} %get-tuple-element.12.p_ref, f32[128,512]{1,0:T(8,128)S(1)} %get-tuple-element.13.g_ref, ...), custom_call_target="tpu_custom_call" | custom-call | tf_op jit(solution)/shard_map/update/pallas_call | solution.py:441
Async XLA Ops:
  0.6 1.0 %copy-start = (f32[256,512]{1,0:T(8,128)S(1)}, f32[256,512]{1,0:T(8,128)}, u32[]{:S(2)}) copy-start(f32[256,512]{1,0:T(8,128)} %slab_hbm.1) | copy-start | bytes 1572868
  1.7 0.9 %copy-start.1 = (f32[144,256]{1,0:T(8,128)S(1)}, f32[144,256]{1,0:T(8,128)}, u32[]{:S(2)}) copy-start(f32[144,256]{1,0:T(8,128)} %sketch_hbm.1) | copy-start | bytes 442372
  2.6 0.7 %copy-start.2 = (s32[1,128]{1,0:T(1,128)S(1)}, s32[1,128]{1,0:T(1,128)}, u32[]{:S(2)}) copy-start(s32[1,128]{1,0:T(1,128)} %piv_hbm.1) | copy-start | bytes 1540

commit v5 on v4

--- a/solution.py
+++ b/solution.py
@@ -9,6 +9,8 @@
 from jax.sharding import PartitionSpec as P
 
 PANEL = 128
+VMEM_REDUCE = 54400 * 1024
+VMEM_UPDATE = 54400 * 1024
 NY = 4
 NZX = 16
 NCOL = 4
@@ -88,13 +90,13 @@
 
 def reduce_kernel(
     slab_hbm, sketch_hbm, piv_hbm,
-    b_ref, p_ref, g_ref, s_ref, r_out, x_out,
-    slab_ref, sketch_ref, piv_ref,
+    b_hbm, p_ref, gfull, s_hbm, r_out, x_out,
+    slab_ref, b_ref, sketch_ref, piv_ref,
     pk, pp, rc1, rc2, leadbuf,
     wpart, wa, wsum, wb, wtot, wfull,
-    gpart, ga, gsum, gb, gfull,
+    gpart, ga, gsum, gb,
     spart, sa, ssum, sb, sbx, sfull,
-    sem_in, sem1, sem_lead, wa_sem, wb_sem, wc_sem, ga_sem, gb_sem, gc_sem, gd_sem,
+    sem_in, sem_out, sem1, sem_lead, wa_sem, wb_sem, wc_sem, ga_sem, gb_sem, gc_sem, gd_sem,
     sa_sem, sb_sem, sbx_sem, sc_sem, sd_sem,
 ):
     r = lax.axis_index("row")
@@ -217,6 +219,8 @@
     lead = jnp.where(c == 0, leadbuf[0], leadbuf[1])
     swapped = swapped_columns(slab, lead, onehot)
     b_ref[...] = swapped
+    store_b = pltpu.make_async_copy(b_ref, b_hbm, sem_out.at[0])
+    store_b.start()
     inner = hdot(panel, swapped, (0, 0))
     for b in range(4):
         gpart[b] = inner[:, 128 * b : 128 * b + 128]
@@ -277,14 +281,18 @@
     delta = (d - l2) + (((e1 + e2) + low) - (l3 + l4))
     gram_two = eye + hdot(hdot(x_one, delta), x_one, (1, 1))
     from_y(lambda t: sfull.at[t], sd_sem)
+    stores = [store_b]
     for b in range(4):
-        s_ref[0, :, 128 * b : 128 * b + 128] = sfull[b]
+        copy = pltpu.make_async_copy(
+            sfull.at[b], s_hbm.at[0, :, 128 * b : 128 * b + 128], sem_out.at[1 + b]
+        )
+        copy.start()
+        stores.append(copy)
     eliminate(gram_two, r_out.at[1], x_out.at[1])
 
     from_y(lambda t: gfull.at[t], gd_sem)
-    for b in range(4):
-        g_ref[:, 128 * b : 128 * b + 128] = gfull[b]
-
+    for copy in stores:
+        copy.wait()
     for copy in pending:
         copy.wait_send()
 
@@ -304,6 +312,21 @@
 
 def spread(v):
     return jnp.broadcast_to(v, (8, 128))
+
+
+def split_three(x):
+    high = x.astype(BF16).astype(F32)
+    rest = x - high
+    mid = rest.astype(BF16).astype(F32)
+    return high, mid, rest - mid
+
+
+def thin_dot(left, right):
+    l0, l1, l2 = split_three(left)
+    r0, r1, r2 = split_three(right)
+    lefts = jnp.concatenate([l0, l0, l1, l0, l1, l2], axis=0).astype(BF16)
+    rights = jnp.concatenate([r0, r1, r0, r2, r1, r0], axis=0).astype(BF16)
+    return bdot(lefts, rights, (0, 0))
 
 
 def block_factor(v, first, sub, lane):
@@ -360,17 +383,19 @@
             updates.append(coef * spread(both[p : p + 1, :]))
         blocks[b + 1] = jnp.where(inside, 0.0, rows) - tree_sum(updates)
         if b + 2 < count:
-            update = hdot(upper, both, (0, 0))
+            update = thin_dot(upper, both)
             for k in range(b + 2, count):
                 blocks[k] = jnp.where(inside, 0.0, blocks[k]) - update[8 * k : 8 * k + 8, :]
 
 
 def update_kernel(
-    b_ref, p_ref, g_ref, s_in, r_ref, x_ref,
+    b_in, p_ref, g_ref, s_in, r_ref, x_ref,
     s_hbm, q_hbm, e_hbm, first_hbm, out_hbm,
-    qbuf, ebuf, fbuf, obuf, sem,
+    b_ref, qbuf, ebuf, fbuf, obuf, sem,
 ):
     lead_block = lax.axis_index("col") == 0
+    load_b = pltpu.make_async_copy(b_in, b_ref, sem.at[8])
+    load_b.start()
     copies = [pltpu.make_async_copy(s_in, s_hbm, sem.at[0])]
     copies[0].start()
     scale = 1.0 / 128.0
@@ -388,9 +413,10 @@
     qbuf[...] = basis * 128.0
     store(2, qbuf, q_hbm.at[0])
     r_factor = hdot(r_ref[1], r_one)
+    load_b.wait()
     for k in range(4):
         cols = slice(128 * k, 128 * k + 128)
-        projected = hdot(inverse, g_ref[:, cols])
+        projected = hdot(inverse, g_ref[k])
         rest = b_ref[:, cols] - hdot(basis, projected)
         if k == 0:
             projected = jnp.where(lead_block, r_factor, projected)
@@ -416,25 +442,26 @@
     swapped, panel, inner, sketches, factors, inverses = pl.pallas_call(
         reduce_kernel,
         out_shape=(
-            flat(rows, width), flat(rows, PANEL), flat(PANEL, width), flat(1, sk, width),
+            flat(rows, width), flat(rows, PANEL), flat(4, PANEL, PANEL), flat(1, sk, width),
             flat(2, PANEL, PANEL), flat(2, PANEL, PANEL),
         ),
         in_specs=[hbm] * 3,
-        out_specs=(VMEM_SPEC,) * 6,
+        out_specs=(hbm, VMEM_SPEC, VMEM_SPEC, hbm, VMEM_SPEC, VMEM_SPEC),
         scratch_shapes=[
-            pltpu.VMEM((rows, width), F32), pltpu.VMEM((sk, rows), F32), pltpu.VMEM((1, PANEL), jnp.int32),
+            pltpu.VMEM((rows, width), F32), pltpu.VMEM((rows, width), F32),
+            pltpu.VMEM((sk, rows), F32), pltpu.VMEM((1, PANEL), jnp.int32),
             pltpu.VMEM((rows, PANEL), F32), pltpu.VMEM((rows, PANEL), F32),
             pltpu.VMEM((rows, PANEL), F32), pltpu.VMEM((rows, PANEL), F32),
             pltpu.VMEM((2, rows, PANEL), F32),
             block(16), block(NY), block(), block(NZX), block(), block(16),
-            square(NY), square(NY), square(), tile(NZX), square(NY),
+            square(NY), square(NY), square(), tile(NZX),
             tall(NY), tall(NY), tall(), tile(NZX), block(NZX), tall(NY),
-            dma((3,)), dma((4,)), dma((4,)), dma((2, NY)), dma((2, NZX)), dma((2, 16)),
+            dma((3,)), dma((5,)), dma((4,)), dma((4,)), dma((2, NY)), dma((2, NZX)), dma((2, 16)),
             dma((2, NY)), dma((2, NZX)), dma((2, NZX)), dma((2, NY)),
             dma((2, NY)), dma((2, NZX)), dma((2, NZX)), dma((2, NZX)), dma((2, NY)),
         ],
         compiler_params=pltpu.CompilerParams(
-            collective_id=0, has_side_effects=True, vmem_limit_bytes=32 * 1024 * 1024
+            collective_id=0, has_side_effects=True, vmem_limit_bytes=VMEM_REDUCE
         ),
         name="reduce",
     )(matrix_slab, sketch_matrix, pivots)
@@ -444,13 +471,13 @@
             flat(1, sk, width), flat(1, rows, PANEL), flat(1, PANEL, width),
             flat(1, PANEL, PANEL), flat(rows, width),
         ),
-        in_specs=[VMEM_SPEC] * 3 + [pl.BlockSpec(memory_space=pl.ANY)] + [VMEM_SPEC] * 2,
+        in_specs=[hbm, VMEM_SPEC, VMEM_SPEC, hbm, VMEM_SPEC, VMEM_SPEC],
         out_specs=(hbm,) * 5,
         scratch_shapes=[
-            pltpu.VMEM((rows, PANEL), F32), pltpu.VMEM((PANEL, width), F32),
-            pltpu.VMEM((PANEL, PANEL), F32), pltpu.VMEM((rows, width), F32), dma((8,)),
+            pltpu.VMEM((rows, width), F32), pltpu.VMEM((rows, PANEL), F32), pltpu.VMEM((PANEL, width), F32),
+            pltpu.VMEM((PANEL, PANEL), F32), pltpu.VMEM((rows, width), F32), dma((9,)),
         ],
-        compiler_params=pltpu.CompilerParams(vmem_limit_bytes=32 * 1024 * 1024),
+        compiler_params=pltpu.CompilerParams(vmem_limit_bytes=VMEM_UPDATE),
         name="update",
     )(swapped, panel, inner, sketches, factors, inverses)
 

time: 52.5 us -> 58.7 us (1.12)
  the two profiles are of different devices: /device:TPU:1 before, /device:TPU:6 now
where the time goes in v5:
time: 58.7 us; the launch traced here: 58.5 us
  Pallas kernels  56.3 us (96%)
  local copies, waits for them, and re-layouts  1.56 us (3%)
  between operations  0.65 us (1%)
    pallas_call x1, Pallas kernels, shards(): pl.pallas_call(reduce_kernel, out_shape=(flat(rows, width), flat(rows, PA...  46.1 us
    pallas_call x1, Pallas kernels, shards(): pl.pallas_call(update_kernel, out_shape=(flat(1, sk, width), flat(1, rows...  10.1 us
    unnamed x4, local copies, waits for them, and re-layouts  1.56 us

profile of v5, /device:TPU:6, one launch (start us, length us, event | category | flops | bytes accessed | tf_op | source)
XLA Modules:
  0.0 58.5 jit_solution(13523881922257371429)
XLA Ops:
  0.6 0.0 copy-start
  0.6 0.9 %copy-done = f32[144,256]{1,0:T(8,128)S(1)} copy-done((f32[144,256]{1,0:T(8,128)S(1)}, f32[144,256]{1,0:T(8,128)}, u32[]{:S(2)}) %copy-start) | copy-done | bytes 147480
  1.5 0.0 copy-start.1
  1.5 0.7 %copy-done.1 = s32[1,128]{1,0:T(1,128)S(1)} copy-done((s32[1,128]{1,0:T(1,128)S(1)}, s32[1,128]{1,0:T(1,128)}, u32[]{:S(2)}) %copy-start.1) | copy-done | bytes 536
  2.2 46.1 %reduce.1 = (f32[256,512]{1,0:T(8,128)}, f32[256,128]{1,0:T(8,128)S(1)}, f32[4,128,128]{2,1,0:T(8,128)S(1)}, f32[1,144,512]{2,1,0:T(8,128)}, f32[2,128,128]{2,1,0:T(8,128)S(1)}, /*index=5*/f32[2,128,128]{2,1,0:T(8,128)S(1)}) custom-call(f32[256,512]{1,0:T(8,128)} %slab_hbm.1, f32[144,256]{1,0:T(8,128)S(1)} %copy-done, s32[1,128]{1,0:T(1,128)S(1)} %copy-done.1), custom_call_target="tpu_custom_call" | custom-call | tf_op jit(solution)/shard_map/reduce/pallas_call | solution.py:442
  48.3 10.1 %update.1 = (f32[1,144,512]{2,1,0:T(8,128)}, f32[1,256,128]{2,1,0:T(8,128)}, f32[1,128,512]{2,1,0:T(8,128)}, f32[1,128,128]{2,1,0:T(8,128)}, f32[256,512]{1,0:T(8,128)}) custom-call(f32[256,512]{1,0:T(8,128)} %get-tuple-element.11.b_in, f32[256,128]{1,0:T(8,128)S(1)} %get-tuple-element.12.p_ref, f32[4,128,128]{2,1,0:T(8,128)S(1)} %get-tuple-element.13.g_ref, ...), custom_call_target="tpu_custom_call" | custom-call | tf_op jit(solution)/shard_map/update/pallas_call | solution.py:468
Async XLA Ops:
  0.6 0.9 %copy-start = (f32[144,256]{1,0:T(8,128)S(1)}, f32[144,256]{1,0:T(8,128)}, u32[]{:S(2)}) copy-start(f32[144,256]{1,0:T(8,128)} %sketch_hbm.1) | copy-start | bytes 442372
  1.5 0.7 %copy-start.1 = (s32[1,128]{1,0:T(1,128)S(1)}, s32[1,128]{1,0:T(1,128)}, u32[]{:S(2)}) copy-start(s32[1,128]{1,0:T(1,128)} %piv_hbm.1) | copy-start | bytes 1540

commit v6 on v4

--- a/solution.py
+++ b/solution.py
@@ -9,6 +9,8 @@
 from jax.sharding import PartitionSpec as P
 
 PANEL = 128
+VMEM_REDUCE = 32 * 1024 * 1024
+VMEM_UPDATE = 32 * 1024 * 1024
 NY = 4
 NZX = 16
 NCOL = 4
@@ -88,12 +90,12 @@
 
 def reduce_kernel(
     slab_hbm, sketch_hbm, piv_hbm,
-    b_ref, p_ref, g_ref, s_ref, r_out, x_out,
+    b_ref, p_ref, gfull, sfull, r_out, x_out,
     slab_ref, sketch_ref, piv_ref,
     pk, pp, rc1, rc2, leadbuf,
     wpart, wa, wsum, wb, wtot, wfull,
-    gpart, ga, gsum, gb, gfull,
-    spart, sa, ssum, sb, sbx, sfull,
+    gpart, ga, gsum, gb,
+    spart, sa, ssum, sb, sbx,
     sem_in, sem1, sem_lead, wa_sem, wb_sem, wc_sem, ga_sem, gb_sem, gc_sem, gd_sem,
     sa_sem, sb_sem, sbx_sem, sc_sem, sd_sem,
 ):
@@ -277,14 +279,9 @@
     delta = (d - l2) + (((e1 + e2) + low) - (l3 + l4))
     gram_two = eye + hdot(hdot(x_one, delta), x_one, (1, 1))
     from_y(lambda t: sfull.at[t], sd_sem)
-    for b in range(4):
-        s_ref[0, :, 128 * b : 128 * b + 128] = sfull[b]
     eliminate(gram_two, r_out.at[1], x_out.at[1])
 
     from_y(lambda t: gfull.at[t], gd_sem)
-    for b in range(4):
-        g_ref[:, 128 * b : 128 * b + 128] = gfull[b]
-
     for copy in pending:
         copy.wait_send()
 
@@ -304,6 +301,21 @@
 
 def spread(v):
     return jnp.broadcast_to(v, (8, 128))
+
+
+def split_three(x):
+    high = x.astype(BF16).astype(F32)
+    rest = x - high
+    mid = rest.astype(BF16).astype(F32)
+    return high, mid, rest - mid
+
+
+def thin_dot(left, right):
+    l0, l1, l2 = split_three(left)
+    r0, r1, r2 = split_three(right)
+    lefts = jnp.concatenate([l0, l0, l1, l0, l1, l2], axis=0).astype(BF16)
+    rights = jnp.concatenate([r0, r1, r0, r2, r1, r0], axis=0).astype(BF16)
+    return bdot(lefts, rights, (0, 0))
 
 
 def block_factor(v, first, sub, lane):
@@ -360,19 +372,18 @@
             updates.append(coef * spread(both[p : p + 1, :]))
         blocks[b + 1] = jnp.where(inside, 0.0, rows) - tree_sum(updates)
         if b + 2 < count:
-            update = hdot(upper, both, (0, 0))
+            update = thin_dot(upper, both)
             for k in range(b + 2, count):
                 blocks[k] = jnp.where(inside, 0.0, blocks[k]) - update[8 * k : 8 * k + 8, :]
 
 
 def update_kernel(
-    b_ref, p_ref, g_ref, s_in, r_ref, x_ref,
+    b_ref, p_ref, g_ref, s_ref, r_ref, x_ref,
     s_hbm, q_hbm, e_hbm, first_hbm, out_hbm,
     qbuf, ebuf, fbuf, obuf, sem,
 ):
     lead_block = lax.axis_index("col") == 0
-    copies = [pltpu.make_async_copy(s_in, s_hbm, sem.at[0])]
-    copies[0].start()
+    copies = []
     scale = 1.0 / 128.0
 
     def store(k, src, dst):
@@ -380,25 +391,27 @@
         copy.start()
         copies.append(copy)
 
+    for k in range(4):
+        store(k, s_ref.at[k], s_hbm.at[0, :, 128 * k : 128 * k + 128])
     r_one = r_ref[0]
     fbuf[...] = r_one * scale
-    store(1, fbuf, first_hbm.at[0])
+    store(8, fbuf, first_hbm.at[0])
     inverse = hdot(x_ref[1], x_ref[0])
     basis = hdot(p_ref[...], inverse, (1, 1))
     qbuf[...] = basis * 128.0
-    store(2, qbuf, q_hbm.at[0])
+    store(9, qbuf, q_hbm.at[0])
     r_factor = hdot(r_ref[1], r_one)
     for k in range(4):
         cols = slice(128 * k, 128 * k + 128)
-        projected = hdot(inverse, g_ref[:, cols])
+        projected = hdot(inverse, g_ref[k])
         rest = b_ref[:, cols] - hdot(basis, projected)
         if k == 0:
             projected = jnp.where(lead_block, r_factor, projected)
             rest = jnp.where(lead_block, 0.0, rest)
         ebuf[:, cols] = projected * scale
         obuf[:, cols] = rest
-        store(3 + k, obuf.at[:, cols], out_hbm.at[:, cols])
-    store(7, ebuf, e_hbm.at[0])
+        store(4 + k, obuf.at[:, cols], out_hbm.at[:, cols])
+    store(10, ebuf, e_hbm.at[0])
     for copy in copies:
         copy.wait()
 
@@ -416,7 +429,7 @@
     swapped, panel, inner, sketches, factors, inverses = pl.pallas_call(
         reduce_kernel,
         out_shape=(
-            flat(rows, width), flat(rows, PANEL), flat(PANEL, width), flat(1, sk, width),
+            flat(rows, width), flat(rows, PANEL), flat(4, PANEL, PANEL), flat(4, sk, PANEL),
             flat(2, PANEL, PANEL), flat(2, PANEL, PANEL),
         ),
         in_specs=[hbm] * 3,
@@ -427,30 +440,30 @@
             pltpu.VMEM((rows, PANEL), F32), pltpu.VMEM((rows, PANEL), F32),
             pltpu.VMEM((2, rows, PANEL), F32),
             block(16), block(NY), block(), block(NZX), block(), block(16),
-            square(NY), square(NY), square(), tile(NZX), square(NY),
-            tall(NY), tall(NY), tall(), tile(NZX), block(NZX), tall(NY),
+            square(NY), square(NY), square(), tile(NZX),
+            tall(NY), tall(NY), tall(), tile(NZX), block(NZX),
             dma((3,)), dma((4,)), dma((4,)), dma((2, NY)), dma((2, NZX)), dma((2, 16)),
             dma((2, NY)), dma((2, NZX)), dma((2, NZX)), dma((2, NY)),
             dma((2, NY)), dma((2, NZX)), dma((2, NZX)), dma((2, NZX)), dma((2, NY)),
         ],
         compiler_params=pltpu.CompilerParams(
-            collective_id=0, has_side_effects=True, vmem_limit_bytes=32 * 1024 * 1024
+            collective_id=0, has_side_effects=True, vmem_limit_bytes=VMEM_REDUCE
         ),
         name="reduce",
-    )(matrix_slab, sketch_matrix, pivots)
+    )(*[pltpu.with_memory_space_constraint(a, pltpu.HBM) for a in (matrix_slab, sketch_matrix, pivots)])
     return pl.pallas_call(
         update_kernel,
         out_shape=(
             flat(1, sk, width), flat(1, rows, PANEL), flat(1, PANEL, width),
             flat(1, PANEL, PANEL), flat(rows, width),
         ),
-        in_specs=[VMEM_SPEC] * 3 + [pl.BlockSpec(memory_space=pl.ANY)] + [VMEM_SPEC] * 2,
+        in_specs=[VMEM_SPEC] * 6,
         out_specs=(hbm,) * 5,
         scratch_shapes=[
             pltpu.VMEM((rows, PANEL), F32), pltpu.VMEM((PANEL, width), F32),
-            pltpu.VMEM((PANEL, PANEL), F32), pltpu.VMEM((rows, width), F32), dma((8,)),
+            pltpu.VMEM((PANEL, PANEL), F32), pltpu.VMEM((rows, width), F32), dma((11,)),
         ],
-        compiler_params=pltpu.CompilerParams(vmem_limit_bytes=32 * 1024 * 1024),
+        compiler_params=pltpu.CompilerParams(vmem_limit_bytes=VMEM_UPDATE),
         name="update",
     )(swapped, panel, inner, sketches, factors, inverses)
 

time: 52.5 us -> 49.1 us (0.935)
  the two profiles are of different devices: /device:TPU:1 before, /device:TPU:6 now
where the time goes in v6:
time: 49.1 us; the launch traced here: 49 us
  Pallas kernels  48.3 us (98%)
  between operations  0.64 us (1%)
    pallas_call x1, Pallas kernels, shards(): pl.pallas_call(reduce_kernel, out_shape=(flat(rows, width), flat(rows, PA...  46.1 us
    pallas_call x1, Pallas kernels, shards(): pl.pallas_call(update_kernel, out_shape=(flat(1, sk, width), flat(1, rows...  2.27 us

profile of v6, /device:TPU:6, one launch (start us, length us, event | category | flops | bytes accessed | tf_op | source)
XLA Modules:
  0.0 49.0 jit_solution(16945517594040030591)
XLA Ops:
  0.6 46.1 %reduce.1 = (f32[256,512]{1,0:T(8,128)S(1)}, f32[256,128]{1,0:T(8,128)S(1)}, f32[4,128,128]{2,1,0:T(8,128)S(1)}, f32[4,144,128]{2,1,0:T(8,128)S(1)}, f32[2,128,1...) custom-call(f32[256,512]{1,0:T(8,128)} %slab_hbm.1, f32[144,256]{1,0:T(8,128)} %sketch_hbm.1, s32[1,128]{1,0:T(1,128)} %piv_hbm.1), custom_call_target="tpu_custom_call" | custom-call | tf_op jit(solution)/shard_map/reduce/pallas_call | solution.py:429
  46.7 2.3 %update.1 = (f32[1,144,512]{2,1,0:T(8,128)}, f32[1,256,128]{2,1,0:T(8,128)}, f32[1,128,512]{2,1,0:T(8,128)}, f32[1,128,128]{2,1,0:T(8,128)}, f32[256,512]{1,0:T(8,128)}) custom-call(f32[256,512]{1,0:T(8,128)S(1)} %get-tuple-element.11.b_ref, f32[256,128]{1,0:T(8,128)S(1)} %get-tuple-element.12.p_ref, f32[4,128,128]{2,1,0:T(8,128)S(1)} %get-tuple-element.13.g_ref, ...), custom_call_target="tpu_custom_call" | custom-call | tf_op jit(solution)/shard_map/update/pallas_call | solution.py:454

commit v7 on v6

--- a/solution.py
+++ b/solution.py
@@ -88,6 +88,30 @@
     )
 
 
+def pack_symmetric(high, low):
+    row = lax.broadcasted_iota(jnp.int32, (64, 128), 0)
+    lane = lax.broadcasted_iota(jnp.int32, (64, 128), 1)
+    join = lambda a, b: jnp.where(lane[: a.shape[0]] < 64, a, pltpu.roll(b, 64, 1))
+    corner = lambda v: jnp.where(row > lane, v[:64], pltpu.roll(v[64:], 64, 1))
+    diagonal = lambda v: jnp.sum(jnp.where(row == lane, v[:64], 0.0), axis=0, keepdims=True)
+    packed = jnp.concatenate([join(high[64:], low[64:]), join(corner(high), corner(low))], axis=0)
+    return packed, join(diagonal(high), diagonal(low))
+
+
+def unpack_symmetric(packed, diagonal):
+    row = lax.broadcasted_iota(jnp.int32, (64, 128), 0)
+    lane = lax.broadcasted_iota(jnp.int32, (64, 128), 1)
+    below, corner = packed[:64], packed[64:]
+    top = jnp.where(row == lane, diagonal, corner)
+    bottom = jnp.where(lane < 64, below, pltpu.roll(corner, 64, 1))
+    part = jnp.concatenate([top, bottom], axis=0)
+    row = lax.broadcasted_iota(jnp.int32, (128, 128), 0)
+    lane = lax.broadcasted_iota(jnp.int32, (128, 128), 1)
+    lower = (lane <= row) & ((row < 64) | (lane < 64))
+    upper = (row >= 64) & (lane >= row)
+    return jnp.where(lower | upper, part, part.T)
+
+
 def reduce_kernel(
     slab_hbm, sketch_hbm, piv_hbm,
     b_ref, p_ref, gfull, sfull, r_out, x_out,
@@ -96,13 +120,16 @@
     wpart, wa, wsum, wb, wtot, wfull,
     gpart, ga, gsum, gb,
     spart, sa, ssum, sb, sbx,
-    sem_in, sem1, sem_lead, wa_sem, wb_sem, wc_sem, ga_sem, gb_sem, gc_sem, gd_sem,
+    sem_in, sem1, sem_p, sem_lead, wa_sem, wb_sem, wc_sem, ga_sem, gb_sem, gc_sem, gd_sem,
     sa_sem, sb_sem, sbx_sem, sc_sem, sd_sem,
 ):
     r = lax.axis_index("row")
     c = lax.axis_index("col")
     y = lax.div(r, NZX)
     w = lax.rem(r, NZX)
+    core = lax.rem(c, 2)
+    other_core = c + 1 - 2 * core
+    other_chip = lax.rem(c + 2, NCOL)
     width = slab_ref.shape[1]
     load_piv = pltpu.make_async_copy(piv_hbm, piv_ref, sem_in.at[0])
     load_slab = pltpu.make_async_copy(slab_hbm, slab_ref, sem_in.at[1])
@@ -113,15 +140,19 @@
 
     y_peers = [(lax.rem(y + i, NY), i) for i in range(1, NY)]
     zx_peers = [lax.rem(w + i, NZX) for i in range(1, NZX)]
-    yc_peers = [
-        (lax.rem(y + i, NY), lax.rem(c + j, NCOL)) for i in range(NY) for j in range(NCOL) if i or j
-    ]
+    own = y * 2 + core
+    pair_peers = [lax.rem(own + i, 2 * NY) for i in range(1, 2 * NY)]
+
+    def pair_device(t):
+        return (lax.div(t, 2) * NZX + w, c - core + lax.rem(t, 2))
 
     barrier = pltpu.get_barrier_semaphore()
     for t in zx_peers:
         pl.semaphore_signal(barrier, inc=1, device_id=(y * NZX + t, c), device_id_type=MESH)
-    for t, d in yc_peers:
-        pl.semaphore_signal(barrier, inc=1, device_id=(t * NZX + w, d), device_id_type=MESH)
+    for t in pair_peers:
+        pl.semaphore_signal(barrier, inc=1, device_id=pair_device(t), device_id_type=MESH)
+    for d in (other_chip, other_chip + 1 - 2 * core):
+        pl.semaphore_signal(barrier, inc=1, device_id=(r, d), device_id_type=MESH)
 
     load_piv.wait()
     onehot = pivot_onehot(piv_ref[...], c * width, width)
@@ -133,7 +164,7 @@
     for b in range(4):
         spart[b] = sketch[:, 128 * b : 128 * b + 128]
     leadbuf[0] = slab[:, :PANEL]
-    pl.semaphore_wait(barrier, NZX - 1 + NY * NCOL - 1)
+    pl.semaphore_wait(barrier, NZX - 1 + 2 * NY - 1 + 2)
 
     pending = []
 
@@ -167,18 +198,18 @@
         for k in range(1, count):
             total, e = two_sum(total, buf[k])
             err = err + e
-        lane16 = lax.broadcasted_iota(jnp.int32, total.shape, 1)
-        return jnp.where(lane16 < 64, total, total + pltpu.roll(err, 64, 1))
-
-    core = c + 1 - 2 * lax.rem(c, 2)
-    chip = lax.rem(c + 2, NCOL)
-    first = remote(pk, rc1, sem1.at[0], sem1.at[1], (r, core))
+        lanes = lax.broadcasted_iota(jnp.int32, total.shape, 1)
+        return jnp.where(lanes < 64, total, total + pltpu.roll(err, 64, 1))
+
+    mine = pl.ds(pl.multiple_of(128 * core, 128), 128)
+    theirs = pl.ds(pl.multiple_of(128 - 128 * core, 128), 128)
+    first = remote(pk.at[theirs], rc1, sem1.at[0], sem1.at[1], (r, other_core))
     first.start()
     to_y(lambda t: spart.at[t], lambda m: sa.at[m], sa_sem)
     sa[y] = spart[y]
     first.wait_recv()
-    pp[...] = pk[...] + rc1[...]
-    second = remote(pp, rc2, sem1.at[2], sem1.at[3], (r, chip))
+    pp[...] = pk[mine] + rc1[...]
+    second = remote(pp, rc2, sem1.at[2], sem1.at[3], (r, other_chip))
     second.start()
     lead_copies = [
         remote(leadbuf.at[0], leadbuf.at[1], sem_lead.at[j - 1], sem_lead.at[3], (r, j)) for j in range(1, NCOL)
@@ -191,19 +222,24 @@
 
     second.wait_recv()
     pending.extend([first, second])
-    panel = pp[...] + rc2[...]
+    half = pp[...] + rc2[...]
+    p_ref[mine] = half
+    third = remote(p_ref.at[mine], p_ref.at[mine], sem_p.at[0], sem_p.at[1], (r, other_core))
+    third.start()
+    pending.append(third)
 
     lane = lax.broadcasted_iota(jnp.int32, (PANEL, PANEL), 1)
-    left = lane < 64
-    l0, l1, l2, l3, l4 = gram_levels(panel)
+    l0, l1, l2, l3, l4 = gram_levels(half)
     high, low = two_sum(l0, l1)
     high, low2 = two_sum(high, l2)
     low = (low + low2) + (l3 + l4)
-    wpart[0:8] = jnp.where(left, high, pltpu.roll(low, 64, 1)).reshape(8, 16, 128)
-    wpart[8:16] = jnp.where(left, pltpu.roll(high, 64, 1), low).reshape(8, 16, 128)
-    to_y(lambda t: wpart.at[c * 4 + t], lambda m: wa.at[m], wa_sem)
-    wa[y] = wpart[c * 4 + y]
-    p_ref[...] = panel
+    packed, diagonal = pack_symmetric(high, low)
+    for o in range(2 * NY):
+        wpart[o, 0:16] = packed[16 * o : 16 * o + 16]
+        wpart[o, 16:17] = diagonal
+    for t in pair_peers:
+        send(wpart.at[t], wa.at[own], wa_sem.at[0, t], wa_sem.at[1, own], pair_device(t))
+    wa[own] = wpart[own]
 
     from_y(lambda t: sa.at[t], sa_sem)
     ssum[...] = total_of(sa, NY)
@@ -217,6 +253,8 @@
         remote(leadbuf.at[0], leadbuf.at[1], sem_lead.at[0], sem_lead.at[3], (r, c)).wait_recv()
 
     lead = jnp.where(c == 0, leadbuf[0], leadbuf[1])
+    remote(p_ref.at[theirs], p_ref.at[theirs], sem_p.at[0], sem_p.at[1], (r, c)).wait_recv()
+    panel = p_ref[...]
     swapped = swapped_columns(slab, lead, onehot)
     b_ref[...] = swapped
     inner = hdot(panel, swapped, (0, 0))
@@ -225,8 +263,9 @@
     to_y(lambda t: gpart.at[t], lambda m: ga.at[m], ga_sem)
     ga[y] = gpart[y]
 
-    from_y(lambda t: wa.at[t], wa_sem)
-    wsum[...] = two_float_total(wa, NY)
+    for t in pair_peers:
+        remote(wa.at[t], wa.at[t], wa_sem.at[0, t], wa_sem.at[1, t], (r, c)).wait_recv()
+    wsum[...] = two_float_total(wa, 2 * NY)
     to_zx(lambda t: wsum, lambda m: wb.at[m], wb_sem)
     wb[w] = wsum[...]
 
@@ -244,10 +283,9 @@
 
     from_zx(lambda t: wb.at[t], wb_sem)
     wtot[...] = two_float_total(wb, NZX)
-    mine = c * 4 + y
-    for t, d in yc_peers:
-        send(wtot, wfull.at[mine], wc_sem.at[0, d * 4 + t], wc_sem.at[1, mine], (t * NZX + w, d))
-    wfull[mine] = wtot[...]
+    for t in pair_peers:
+        send(wtot, wfull.at[own], wc_sem.at[0, t], wc_sem.at[1, own], pair_device(t))
+    wfull[own] = wtot[...]
 
     from_zx(lambda t: sfull.at[y, tile(t)], sc_sem)
     to_y(lambda t: sfull.at[y], lambda m: sfull.at[m], sd_sem)
@@ -256,13 +294,12 @@
     gfull[y, tile(w)] = total_of(gb, NZX)
     to_zx(lambda t: gfull.at[y, tile(w)], lambda m: gfull.at[y, tile(m)], gc_sem)
 
-    for t, d in yc_peers:
-        o = d * 4 + t
-        remote(wfull.at[o], wfull.at[o], wc_sem.at[0, o], wc_sem.at[1, o], (r, c)).wait_recv()
-    first_half = wfull[0:8].reshape(PANEL, PANEL)
-    second_half = wfull[8:16].reshape(PANEL, PANEL)
-    high = jnp.where(left, first_half, pltpu.roll(second_half, 64, 1))
-    low = jnp.where(left, pltpu.roll(first_half, 64, 1), second_half)
+    for t in pair_peers:
+        remote(wfull.at[t], wfull.at[t], wc_sem.at[0, t], wc_sem.at[1, t], (r, c)).wait_recv()
+    packed = jnp.concatenate([wfull[o, 0:16] for o in range(2 * NY)], axis=0)
+    diagonal = wfull[0, 16:17]
+    high = unpack_symmetric(packed, diagonal)
+    low = unpack_symmetric(pltpu.roll(packed, 64, 1), pltpu.roll(diagonal, 64, 1))
 
     eliminate(high, r_out.at[0], x_out.at[0])
     r_one = r_out[0]
@@ -423,6 +460,7 @@
     hbm = pl.BlockSpec(memory_space=pltpu.HBM)
     tile = lambda *lead: pltpu.VMEM(lead + (8, 128), F32)
     block = lambda *lead: pltpu.VMEM(lead + (16, 128), F32)
+    part = lambda *lead: pltpu.VMEM(lead + (17, 128), F32)
     square = lambda *lead: pltpu.VMEM(lead + (PANEL, 128), F32)
     tall = lambda *lead: pltpu.VMEM(lead + (sk, 128), F32)
     flat = lambda *shape: jax.ShapeDtypeStruct(shape, F32)
@@ -436,13 +474,12 @@
         out_specs=(VMEM_SPEC,) * 6,
         scratch_shapes=[
             pltpu.VMEM((rows, width), F32), pltpu.VMEM((sk, rows), F32), pltpu.VMEM((1, PANEL), jnp.int32),
-            pltpu.VMEM((rows, PANEL), F32), pltpu.VMEM((rows, PANEL), F32),
-            pltpu.VMEM((rows, PANEL), F32), pltpu.VMEM((rows, PANEL), F32),
+            pltpu.VMEM((rows, PANEL), F32), square(), square(), square(),
             pltpu.VMEM((2, rows, PANEL), F32),
-            block(16), block(NY), block(), block(NZX), block(), block(16),
+            part(2 * NY), part(2 * NY), part(), part(NZX), part(), part(2 * NY),
             square(NY), square(NY), square(), tile(NZX),
             tall(NY), tall(NY), tall(), tile(NZX), block(NZX),
-            dma((3,)), dma((4,)), dma((4,)), dma((2, NY)), dma((2, NZX)), dma((2, 16)),
+            dma((3,)), dma((4,)), dma((2,)), dma((4,)), dma((2, 2 * NY)), dma((2, NZX)), dma((2, 2 * NY)),
             dma((2, NY)), dma((2, NZX)), dma((2, NZX)), dma((2, NY)),
             dma((2, NY)), dma((2, NZX)), dma((2, NZX)), dma((2, NZX)), dma((2, NY)),
         ],

time: 49.1 us -> 47.7 us (0.971)
  Pallas kernels: 48.3 us -> 47 us
    pallas_call x1, Pallas kernels: 46.1 us -> 44.7 us  [shards(): pl.pallas_call(reduce_kernel, out_shape=(flat(rows, width), flat(rows, PA...]
where the time goes in v7:
time: 47.7 us; the launch traced here: 47.6 us
  Pallas kernels  47 us (99%)
  between operations  0.64 us (1%)
    pallas_call x1, Pallas kernels, shards(): pl.pallas_call(reduce_kernel, out_shape=(flat(rows, width), flat(rows, PA...  44.7 us
    pallas_call x1, Pallas kernels, shards(): pl.pallas_call(update_kernel, out_shape=(flat(1, sk, width), flat(1, rows...  2.27 us

profile of v7, /device:TPU:6, one launch (start us, length us, event | category | flops | bytes accessed | tf_op | source)
XLA Modules:
  0.0 47.6 jit_solution(1000720149773926915)
XLA Ops:
  0.6 44.7 %reduce.1 = (f32[256,512]{1,0:T(8,128)S(1)}, f32[256,128]{1,0:T(8,128)S(1)}, f32[4,128,128]{2,1,0:T(8,128)S(1)}, f32[4,144,128]{2,1,0:T(8,128)S(1)}, f32[2,128,1...) custom-call(f32[256,512]{1,0:T(8,128)} %slab_hbm.1, f32[144,256]{1,0:T(8,128)} %sketch_hbm.1, s32[1,128]{1,0:T(1,128)} %piv_hbm.1), custom_call_target="tpu_custom_call" | custom-call | tf_op jit(solution)/shard_map/reduce/pallas_call | solution.py:467
  45.4 2.3 %update.1 = (f32[1,144,512]{2,1,0:T(8,128)}, f32[1,256,128]{2,1,0:T(8,128)}, f32[1,128,512]{2,1,0:T(8,128)}, f32[1,128,128]{2,1,0:T(8,128)}, f32[256,512]{1,0:T(8,128)}) custom-call(f32[256,512]{1,0:T(8,128)S(1)} %get-tuple-element.11.b_ref, f32[256,128]{1,0:T(8,128)S(1)} %get-tuple-element.12.p_ref, f32[4,128,128]{2,1,0:T(8,128)S(1)} %get-tuple-element.13.g_ref, ...), custom_call_target="tpu_custom_call" | custom-call | tf_op jit(solution)/shard_map/update/pallas_call | solution.py:491

commit v8 on v7

--- a/solution.py
+++ b/solution.py
@@ -119,9 +119,9 @@
     pk, pp, rc1, rc2, leadbuf,
     wpart, wa, wsum, wb, wtot, wfull,
     gpart, ga, gsum, gb,
-    spart, sa, ssum, sb, sbx,
-    sem_in, sem1, sem_p, sem_lead, wa_sem, wb_sem, wc_sem, ga_sem, gb_sem, gc_sem, gd_sem,
-    sa_sem, sb_sem, sbx_sem, sc_sem, sd_sem,
+    spart, sa, ssum, sb,
+    sem_in, sem1, sem_p, sem_lead, wa_sem, wb_sem, wc_sem, ga_sem, gb_sem, gc_sem,
+    sa_sem, sb_sem, sc_sem, sd_sem, relay,
 ):
     r = lax.axis_index("row")
     c = lax.axis_index("col")
@@ -147,7 +147,9 @@
         return (lax.div(t, 2) * NZX + w, c - core + lax.rem(t, 2))
 
     barrier = pltpu.get_barrier_semaphore()
-    for t in zx_peers:
+    z_step = lambda k: lax.rem(w + 2 * k + NZX, NZX)
+    across = w + 1 - 2 * lax.rem(w, 2)
+    for t in (z_step(2), z_step(-2), across, z_step(1), z_step(-1)):
         pl.semaphore_signal(barrier, inc=1, device_id=(y * NZX + t, c), device_id_type=MESH)
     for t in pair_peers:
         pl.semaphore_signal(barrier, inc=1, device_id=pair_device(t), device_id_type=MESH)
@@ -164,7 +166,9 @@
     for b in range(4):
         spart[b] = sketch[:, 128 * b : 128 * b + 128]
     leadbuf[0] = slab[:, :PANEL]
-    pl.semaphore_wait(barrier, NZX - 1 + 2 * NY - 1 + 2)
+    pl.semaphore_wait(barrier, 5 + 2 * NY - 1 + 2)
+    for t in (z_step(2), z_step(-2)):
+        pl.semaphore_signal(relay.at[0], inc=1, device_id=(y * NZX + t, c), device_id_type=MESH)
 
     pending = []
 
@@ -228,6 +232,9 @@
     third.start()
     pending.append(third)
 
+    pl.semaphore_wait(relay.at[0], 2)
+    pl.semaphore_signal(relay.at[1], inc=1, device_id=(y * NZX + across, c), device_id_type=MESH)
+
     lane = lax.broadcasted_iota(jnp.int32, (PANEL, PANEL), 1)
     l0, l1, l2, l3, l4 = gram_levels(half)
     high, low = two_sum(l0, l1)
@@ -241,13 +248,6 @@
         send(wpart.at[t], wa.at[own], wa_sem.at[0, t], wa_sem.at[1, own], pair_device(t))
     wa[own] = wpart[own]
 
-    from_y(lambda t: sa.at[t], sa_sem)
-    ssum[...] = total_of(sa, NY)
-    to_zx(lambda t: ssum.at[pl.ds(8 * t, 8)], lambda m: sb.at[m], sb_sem)
-    to_zx(lambda t: ssum.at[pl.ds(128, 16)], lambda m: sbx.at[m], sbx_sem)
-    sb[w] = ssum[pl.ds(pl.multiple_of(8 * w, 8), 8)]
-    sbx[w] = ssum[pl.ds(128, 16)]
-
     @pl.when(c != 0)
     def _():
         remote(leadbuf.at[0], leadbuf.at[1], sem_lead.at[0], sem_lead.at[3], (r, c)).wait_recv()
@@ -266,16 +266,18 @@
     for t in pair_peers:
         remote(wa.at[t], wa.at[t], wa_sem.at[0, t], wa_sem.at[1, t], (r, c)).wait_recv()
     wsum[...] = two_float_total(wa, 2 * NY)
+    pl.semaphore_wait(relay.at[1], 1)
     to_zx(lambda t: wsum, lambda m: wb.at[m], wb_sem)
     wb[w] = wsum[...]
 
-    from_zx(lambda t: sb.at[t], sb_sem)
-    from_zx(lambda t: sbx.at[t], sbx_sem)
+    from_y(lambda t: sa.at[t], sa_sem)
+    total = total_of(sa, NY)
+    for k in range(NZX):
+        ssum[k] = total[9 * k : 9 * k + 9]
+    to_zx(lambda t: ssum.at[t], lambda m: sb.at[m], sb_sem)
+    sb[w] = ssum[w]
+
     tile = lambda t: pl.ds(pl.multiple_of(8 * t, 8), 8)
-    sfull[y, tile(w)] = total_of(sb, NZX)
-    sfull[y, pl.ds(128, 16)] = total_of(sbx, NZX)
-    to_zx(lambda t: sfull.at[y, tile(w)], lambda m: sfull.at[y, tile(m)], sc_sem)
-
     from_y(lambda t: ga.at[t], ga_sem)
     gsum[...] = total_of(ga, NY)
     to_zx(lambda t: gsum.at[tile(t)], lambda m: gb.at[m], gb_sem)
@@ -287,12 +289,9 @@
         send(wtot, wfull.at[own], wc_sem.at[0, t], wc_sem.at[1, own], pair_device(t))
     wfull[own] = wtot[...]
 
-    from_zx(lambda t: sfull.at[y, tile(t)], sc_sem)
-    to_y(lambda t: sfull.at[y], lambda m: sfull.at[m], sd_sem)
-
-    from_zx(lambda t: gb.at[t], gb_sem)
-    gfull[y, tile(w)] = total_of(gb, NZX)
-    to_zx(lambda t: gfull.at[y, tile(w)], lambda m: gfull.at[y, tile(m)], gc_sem)
+    from_zx(lambda t: sb.at[t], sb_sem)
+    sfull[y, w] = total_of(sb, NZX)
+    to_zx(lambda t: sfull.at[y, w], lambda m: sfull.at[y, m], sc_sem)
 
     for t in pair_peers:
         remote(wfull.at[t], wfull.at[t], wc_sem.at[0, t], wc_sem.at[1, t], (r, c)).wait_recv()
@@ -301,12 +300,18 @@
     high = unpack_symmetric(packed, diagonal)
     low = unpack_symmetric(pltpu.roll(packed, 64, 1), pltpu.roll(diagonal, 64, 1))
 
+    from_zx(lambda t: gb.at[t], gb_sem)
+    gfull[y, tile(w)] = total_of(gb, NZX)
+    row_peers = [lax.rem(r + i, NY * NZX) for i in range(1, NY * NZX)]
+    for t in row_peers:
+        send(gfull.at[y, tile(w)], gfull.at[y, tile(w)], gc_sem.at[0, t], gc_sem.at[1, r], (t, c))
+
     eliminate(high, r_out.at[0], x_out.at[0])
     r_one = r_out[0]
     x_one = x_out[0]
 
-    from_zx(lambda t: gfull.at[y, tile(t)], gc_sem)
-    to_y(lambda t: gfull.at[y], lambda m: gfull.at[m], gd_sem)
+    from_zx(lambda t: sfull.at[y, t], sc_sem)
+    to_y(lambda t: sfull.at[y], lambda m: sfull.at[m], sd_sem)
 
     rowi = lax.broadcasted_iota(jnp.int32, (PANEL, PANEL), 0)
     eye = jnp.where(rowi == lane, 1.0, 0.0).astype(F32)
@@ -315,10 +320,12 @@
     d, e2 = two_sum(d, -l1)
     delta = (d - l2) + (((e1 + e2) + low) - (l3 + l4))
     gram_two = eye + hdot(hdot(x_one, delta), x_one, (1, 1))
+    eliminate(gram_two, r_out.at[1], x_out.at[1])
+
     from_y(lambda t: sfull.at[t], sd_sem)
-    eliminate(gram_two, r_out.at[1], x_out.at[1])
-
-    from_y(lambda t: gfull.at[t], gd_sem)
+    for t in row_peers:
+        piece = gfull.at[lax.div(t, NZX), tile(lax.rem(t, NZX))]
+        remote(piece, piece, gc_sem.at[0, t], gc_sem.at[1, t], (r, c)).wait_recv()
     for copy in pending:
         copy.wait_send()
 
@@ -417,7 +424,7 @@
 def update_kernel(
     b_ref, p_ref, g_ref, s_ref, r_ref, x_ref,
     s_hbm, q_hbm, e_hbm, first_hbm, out_hbm,
-    qbuf, ebuf, fbuf, obuf, sem,
+    sbuf, qbuf, ebuf, fbuf, obuf, sem,
 ):
     lead_block = lax.axis_index("col") == 0
     copies = []
@@ -429,7 +436,9 @@
         copies.append(copy)
 
     for k in range(4):
-        store(k, s_ref.at[k], s_hbm.at[0, :, 128 * k : 128 * k + 128])
+        for t in range(NZX):
+            sbuf[9 * t : 9 * t + 9, 128 * k : 128 * k + 128] = s_ref[k, t]
+    store(0, sbuf, s_hbm.at[0])
     r_one = r_ref[0]
     fbuf[...] = r_one * scale
     store(8, fbuf, first_hbm.at[0])
@@ -459,7 +468,7 @@
     dma = pltpu.SemaphoreType.DMA
     hbm = pl.BlockSpec(memory_space=pltpu.HBM)
     tile = lambda *lead: pltpu.VMEM(lead + (8, 128), F32)
-    block = lambda *lead: pltpu.VMEM(lead + (16, 128), F32)
+    nine = lambda *lead: pltpu.VMEM(lead + (9, 128), F32)
     part = lambda *lead: pltpu.VMEM(lead + (17, 128), F32)
     square = lambda *lead: pltpu.VMEM(lead + (PANEL, 128), F32)
     tall = lambda *lead: pltpu.VMEM(lead + (sk, 128), F32)
@@ -467,7 +476,7 @@
     swapped, panel, inner, sketches, factors, inverses = pl.pallas_call(
         reduce_kernel,
         out_shape=(
-            flat(rows, width), flat(rows, PANEL), flat(4, PANEL, PANEL), flat(4, sk, PANEL),
+            flat(rows, width), flat(rows, PANEL), flat(4, PANEL, PANEL), flat(4, NZX, sk // NZX, PANEL),
             flat(2, PANEL, PANEL), flat(2, PANEL, PANEL),
         ),
         in_specs=[hbm] * 3,
@@ -478,10 +487,10 @@
             pltpu.VMEM((2, rows, PANEL), F32),
             part(2 * NY), part(2 * NY), part(), part(NZX), part(), part(2 * NY),
             square(NY), square(NY), square(), tile(NZX),
-            tall(NY), tall(NY), tall(), tile(NZX), block(NZX),
+            tall(NY), tall(NY), nine(NZX), nine(NZX),
             dma((3,)), dma((4,)), dma((2,)), dma((4,)), dma((2, 2 * NY)), dma((2, NZX)), dma((2, 2 * NY)),
-            dma((2, NY)), dma((2, NZX)), dma((2, NZX)), dma((2, NY)),
-            dma((2, NY)), dma((2, NZX)), dma((2, NZX)), dma((2, NZX)), dma((2, NY)),
+            dma((2, NY)), dma((2, NZX)), dma((2, NY * NZX)),
+            dma((2, NY)), dma((2, NZX)), dma((2, NZX)), dma((2, NY)), pltpu.SemaphoreType.REGULAR((2,)),
         ],
         compiler_params=pltpu.CompilerParams(
             collective_id=0, has_side_effects=True, vmem_limit_bytes=VMEM_REDUCE
@@ -497,7 +506,7 @@
         in_specs=[VMEM_SPEC] * 6,
         out_specs=(hbm,) * 5,
         scratch_shapes=[
-            pltpu.VMEM((rows, PANEL), F32), pltpu.VMEM((PANEL, width), F32),
+            pltpu.VMEM((sk, width), F32), pltpu.VMEM((rows, PANEL), F32), pltpu.VMEM((PANEL, width), F32),
             pltpu.VMEM((PANEL, PANEL), F32), pltpu.VMEM((rows, width), F32), dma((11,)),
         ],
         compiler_params=pltpu.CompilerParams(vmem_limit_bytes=VMEM_UPDATE),

time: 47.7 us -> 48 us (level)
  the two profiles are of different devices: /device:TPU:6 before, /device:TPU:1 now
where the time goes in v8:
time: 48 us; the launch traced here: 47.9 us
  Pallas kernels  47.2 us (98%)
  between operations  0.64 us (1%)
    pallas_call x1, Pallas kernels, shards(): pl.pallas_call(reduce_kernel, out_shape=(flat(rows, width), flat(rows, PA...  44.9 us
    pallas_call x1, Pallas kernels, shards(): pl.pallas_call(update_kernel, out_shape=(flat(1, sk, width), flat(1, rows...  2.3 us

profile of v8, /device:TPU:1, one launch (start us, length us, event | category | flops | bytes accessed | tf_op | source)
XLA Modules:
  0.0 47.9 jit_solution(5527468351572868076)
XLA Ops:
  0.6 44.9 %reduce.1 = (f32[256,512]{1,0:T(8,128)S(1)}, f32[256,128]{1,0:T(8,128)S(1)}, f32[4,128,128]{2,1,0:T(8,128)S(1)}, f32[4,16,9,128]{3,2,1,0:T(8,128)S(1)}, f32[2,12...) custom-call(f32[256,512]{1,0:T(8,128)} %slab_hbm.1, f32[144,256]{1,0:T(8,128)} %sketch_hbm.1, s32[1,128]{1,0:T(1,128)} %piv_hbm.1), custom_call_target="tpu_custom_call" | custom-call | tf_op jit(solution)/shard_map/reduce/pallas_call | solution.py:476
  45.6 2.3 %update.1 = (f32[1,144,512]{2,1,0:T(8,128)}, f32[1,256,128]{2,1,0:T(8,128)}, f32[1,128,512]{2,1,0:T(8,128)}, f32[1,128,128]{2,1,0:T(8,128)}, f32[256,512]{1,0:T(8,128)}) custom-call(f32[256,512]{1,0:T(8,128)S(1)} %get-tuple-element.11.b_ref, f32[256,128]{1,0:T(8,128)S(1)} %get-tuple-element.12.p_ref, f32[4,128,128]{2,1,0:T(8,128)S(1)} %get-tuple-element.13.g_ref, ...), custom_call_target="tpu_custom_call" | custom-call | tf_op jit(solution)/shard_map/update/pallas_call | solution.py:500

commit v9 on v8

--- a/solution.py
+++ b/solution.py
@@ -263,13 +263,7 @@
     to_y(lambda t: gpart.at[t], lambda m: ga.at[m], ga_sem)
     ga[y] = gpart[y]
 
-    for t in pair_peers:
-        remote(wa.at[t], wa.at[t], wa_sem.at[0, t], wa_sem.at[1, t], (r, c)).wait_recv()
-    wsum[...] = two_float_total(wa, 2 * NY)
     pl.semaphore_wait(relay.at[1], 1)
-    to_zx(lambda t: wsum, lambda m: wb.at[m], wb_sem)
-    wb[w] = wsum[...]
-
     from_y(lambda t: sa.at[t], sa_sem)
     total = total_of(sa, NY)
     for k in range(NZX):
@@ -277,21 +271,27 @@
     to_zx(lambda t: ssum.at[t], lambda m: sb.at[m], sb_sem)
     sb[w] = ssum[w]
 
+    for t in pair_peers:
+        remote(wa.at[t], wa.at[t], wa_sem.at[0, t], wa_sem.at[1, t], (r, c)).wait_recv()
+    wsum[...] = two_float_total(wa, 2 * NY)
+    to_zx(lambda t: wsum, lambda m: wb.at[m], wb_sem)
+    wb[w] = wsum[...]
+
     tile = lambda t: pl.ds(pl.multiple_of(8 * t, 8), 8)
     from_y(lambda t: ga.at[t], ga_sem)
     gsum[...] = total_of(ga, NY)
     to_zx(lambda t: gsum.at[tile(t)], lambda m: gb.at[m], gb_sem)
     gb[w] = gsum[tile(w)]
 
+    from_zx(lambda t: sb.at[t], sb_sem)
+    sfull[y, w] = total_of(sb, NZX)
+    to_zx(lambda t: sfull.at[y, w], lambda m: sfull.at[y, m], sc_sem)
+
     from_zx(lambda t: wb.at[t], wb_sem)
     wtot[...] = two_float_total(wb, NZX)
     for t in pair_peers:
         send(wtot, wfull.at[own], wc_sem.at[0, t], wc_sem.at[1, own], pair_device(t))
     wfull[own] = wtot[...]
-
-    from_zx(lambda t: sb.at[t], sb_sem)
-    sfull[y, w] = total_of(sb, NZX)
-    to_zx(lambda t: sfull.at[y, w], lambda m: sfull.at[y, m], sc_sem)
 
     for t in pair_peers:
         remote(wfull.at[t], wfull.at[t], wc_sem.at[0, t], wc_sem.at[1, t], (r, c)).wait_recv()
@@ -306,12 +306,13 @@
     for t in row_peers:
         send(gfull.at[y, tile(w)], gfull.at[y, tile(w)], gc_sem.at[0, t], gc_sem.at[1, r], (t, c))
 
-    eliminate(high, r_out.at[0], x_out.at[0])
+    def sketch_home():
+        from_zx(lambda t: sfull.at[y, t], sc_sem)
+        to_y(lambda t: sfull.at[y], lambda m: sfull.at[m], sd_sem)
+
+    eliminate(high, r_out.at[0], x_out.at[0], {4: sketch_home})
     r_one = r_out[0]
     x_one = x_out[0]
-
-    from_zx(lambda t: sfull.at[y, t], sc_sem)
-    to_y(lambda t: sfull.at[y], lambda m: sfull.at[m], sd_sem)
 
     rowi = lax.broadcasted_iota(jnp.int32, (PANEL, PANEL), 0)
     eye = jnp.where(rowi == lane, 1.0, 0.0).astype(F32)
@@ -394,12 +395,14 @@
     return solved, jnp.where(inside, inverse, solved), m
 
 
-def eliminate(w, r_ref, x_ref):
+def eliminate(w, r_ref, x_ref, between={}):
     sub = lax.broadcasted_iota(jnp.int32, (8, 128), 0)
     lane = lax.broadcasted_iota(jnp.int32, (8, 128), 1)
     count = PANEL // 8
     blocks = [w[8 * b : 8 * b + 8, :] for b in range(count)]
     for b in range(count):
+        if b in between:
+            between[b]()
         first = 8 * b
         solved, both, m = block_factor(blocks[b], first, sub, lane)
         upper = jnp.where(lane >= first + sub, solved, 0.0)

time: 48 us -> 46.2 us (0.963)
  Pallas kernels: 47.2 us -> 45.5 us
    pallas_call x1, Pallas kernels: 44.9 us -> 43.2 us  [shards(): pl.pallas_call(reduce_kernel, out_shape=(flat(rows, width), flat(rows, PA...]
where the time goes in v9:
time: 46.2 us; the launch traced here: 46.1 us
  Pallas kernels  45.5 us (98%)
  between operations  0.64 us (1%)
    pallas_call x1, Pallas kernels, shards(): pl.pallas_call(reduce_kernel, out_shape=(flat(rows, width), flat(rows, PA...  43.2 us
    pallas_call x1, Pallas kernels, shards(): pl.pallas_call(update_kernel, out_shape=(flat(1, sk, width), flat(1, rows...  2.3 us

profile of v9, /device:TPU:1, one launch (start us, length us, event | category | flops | bytes accessed | tf_op | source)
XLA Modules:
  0.0 46.1 jit_solution(4279482554915333262)
XLA Ops:
  0.6 43.2 %reduce.1 = (f32[256,512]{1,0:T(8,128)S(1)}, f32[256,128]{1,0:T(8,128)S(1)}, f32[4,128,128]{2,1,0:T(8,128)S(1)}, f32[4,16,9,128]{3,2,1,0:T(8,128)S(1)}, f32[2,12...) custom-call(f32[256,512]{1,0:T(8,128)} %slab_hbm.1, f32[144,256]{1,0:T(8,128)} %sketch_hbm.1, s32[1,128]{1,0:T(1,128)} %piv_hbm.1), custom_call_target="tpu_custom_call" | custom-call | tf_op jit(solution)/shard_map/reduce/pallas_call | solution.py:479
  43.8 2.3 %update.1 = (f32[1,144,512]{2,1,0:T(8,128)}, f32[1,256,128]{2,1,0:T(8,128)}, f32[1,128,512]{2,1,0:T(8,128)}, f32[1,128,128]{2,1,0:T(8,128)}, f32[256,512]{1,0:T(8,128)}) custom-call(f32[256,512]{1,0:T(8,128)S(1)} %get-tuple-element.11.b_ref, f32[256,128]{1,0:T(8,128)S(1)} %get-tuple-element.12.p_ref, f32[4,128,128]{2,1,0:T(8,128)S(1)} %get-tuple-element.13.g_ref, ...), custom_call_target="tpu_custom_call" | custom-call | tf_op jit(solution)/shard_map/update/pallas_call | solution.py:503

commit v10 on v9

--- a/solution.py
+++ b/solution.py
@@ -114,8 +114,8 @@
 
 def reduce_kernel(
     slab_hbm, sketch_hbm, piv_hbm,
-    b_ref, p_ref, gfull, sfull, r_out, x_out,
-    slab_ref, sketch_ref, piv_ref,
+    b_ref, q_ref, gfull, sfull, first_ref, rfac_ref, inv_ref,
+    slab_ref, sketch_ref, piv_ref, p_ref, r_out, x_out, held,
     pk, pp, rc1, rc2, leadbuf,
     wpart, wa, wsum, wb, wtot, wfull,
     gpart, ga, gsum, gb,
@@ -310,7 +310,7 @@
         from_zx(lambda t: sfull.at[y, t], sc_sem)
         to_y(lambda t: sfull.at[y], lambda m: sfull.at[m], sd_sem)
 
-    eliminate(high, r_out.at[0], x_out.at[0], {4: sketch_home})
+    eliminate(high, r_out.at[0], x_out.at[0], held, {4: sketch_home})
     r_one = r_out[0]
     x_one = x_out[0]
 
@@ -321,7 +321,13 @@
     d, e2 = two_sum(d, -l1)
     delta = (d - l2) + (((e1 + e2) + low) - (l3 + l4))
     gram_two = eye + hdot(hdot(x_one, delta), x_one, (1, 1))
-    eliminate(gram_two, r_out.at[1], x_out.at[1])
+    eliminate(gram_two, r_out.at[1], x_out.at[1], held)
+
+    inverse = hdot(x_out[1], x_out[0])
+    inv_ref[...] = inverse
+    q_ref[...] = hdot(p_ref[...], inverse, (1, 1))
+    first_ref[...] = r_out[0] * (1.0 / 128.0)
+    rfac_ref[...] = hdot(r_out[1], r_out[0])
 
     from_y(lambda t: sfull.at[t], sd_sem)
     for t in row_peers:
@@ -363,9 +369,11 @@
     return bdot(lefts, rights, (0, 0))
 
 
-def block_factor(v, first, sub, lane):
-    columns = [spread(v[:, first + j : first + j + 1]) for j in range(8)]
-    a = {(i, j): spread(columns[i][j : j + 1, :]) for j in range(8) for i in range(j + 1)}
+def block_factor(v, columns, held, first, sub, lane):
+    slot = first % 16
+    for i in range(8):
+        held[slot + i] = columns[i]
+    a = {(i, j): held[slot + i, pl.ds(j, 8, stride=0), :] for j in range(8) for i in range(j + 1)}
     m = [[None] * 8 for _ in range(8)]
     for i in range(8):
         inv = lax.rsqrt(a[i, i])
@@ -395,16 +403,17 @@
     return solved, jnp.where(inside, inverse, solved), m
 
 
-def eliminate(w, r_ref, x_ref, between={}):
+def eliminate(w, r_ref, x_ref, held, between={}):
     sub = lax.broadcasted_iota(jnp.int32, (8, 128), 0)
     lane = lax.broadcasted_iota(jnp.int32, (8, 128), 1)
     count = PANEL // 8
     blocks = [w[8 * b : 8 * b + 8, :] for b in range(count)]
+    spread_next = [spread(blocks[0][:, j : j + 1]) for j in range(8)]
     for b in range(count):
         if b in between:
             between[b]()
         first = 8 * b
-        solved, both, m = block_factor(blocks[b], first, sub, lane)
+        solved, both, m = block_factor(blocks[b], spread_next, held, first, sub, lane)
         upper = jnp.where(lane >= first + sub, solved, 0.0)
         r_ref[first : first + 8, :] = upper
         x_ref[first : first + 8, :] = jnp.where(lane < first + 8, both, 0.0)
@@ -413,11 +422,17 @@
         inside = (lane >= first) & (lane < first + 8)
         rows = blocks[b + 1]
         columns = [spread(rows[:, first + j : first + j + 1]) for j in range(8)]
-        updates = []
+        updates, coefs = [], []
         for p in range(8):
             coef = tree_sum([m[p][j] * columns[j] for j in range(p + 1)])
+            coefs.append(coef)
             updates.append(coef * spread(both[p : p + 1, :]))
         blocks[b + 1] = jnp.where(inside, 0.0, rows) - tree_sum(updates)
+        spread_next = [
+            spread(rows[:, first + 8 + j : first + 9 + j])
+            - tree_sum([coefs[p] * spread(coefs[p][j : j + 1, :]) for p in range(8)])
+            for j in range(8)
+        ]
         if b + 2 < count:
             update = thin_dot(upper, both)
             for k in range(b + 2, count):
@@ -425,9 +440,9 @@
 
 
 def update_kernel(
-    b_ref, p_ref, g_ref, s_ref, r_ref, x_ref,
+    b_ref, q_ref, g_ref, s_ref, first_ref, rfac_ref, inv_ref,
     s_hbm, q_hbm, e_hbm, first_hbm, out_hbm,
-    sbuf, qbuf, ebuf, fbuf, obuf, sem,
+    sbuf, qbuf, ebuf, obuf, sem,
 ):
     lead_block = lax.axis_index("col") == 0
     copies = []
@@ -442,14 +457,12 @@
         for t in range(NZX):
             sbuf[9 * t : 9 * t + 9, 128 * k : 128 * k + 128] = s_ref[k, t]
     store(0, sbuf, s_hbm.at[0])
-    r_one = r_ref[0]
-    fbuf[...] = r_one * scale
-    store(8, fbuf, first_hbm.at[0])
-    inverse = hdot(x_ref[1], x_ref[0])
-    basis = hdot(p_ref[...], inverse, (1, 1))
+    store(8, first_ref, first_hbm.at[0])
+    basis = q_ref[...]
     qbuf[...] = basis * 128.0
     store(9, qbuf, q_hbm.at[0])
-    r_factor = hdot(r_ref[1], r_one)
+    r_factor = rfac_ref[...]
+    inverse = inv_ref[...]
     for k in range(4):
         cols = slice(128 * k, 128 * k + 128)
         projected = hdot(inverse, g_ref[k])
@@ -476,16 +489,17 @@
     square = lambda *lead: pltpu.VMEM(lead + (PANEL, 128), F32)
     tall = lambda *lead: pltpu.VMEM(lead + (sk, 128), F32)
     flat = lambda *shape: jax.ShapeDtypeStruct(shape, F32)
-    swapped, panel, inner, sketches, factors, inverses = pl.pallas_call(
+    mid = pl.pallas_call(
         reduce_kernel,
         out_shape=(
             flat(rows, width), flat(rows, PANEL), flat(4, PANEL, PANEL), flat(4, NZX, sk // NZX, PANEL),
-            flat(2, PANEL, PANEL), flat(2, PANEL, PANEL),
+            flat(PANEL, PANEL), flat(PANEL, PANEL), flat(PANEL, PANEL),
         ),
         in_specs=[hbm] * 3,
-        out_specs=(VMEM_SPEC,) * 6,
+        out_specs=(VMEM_SPEC,) * 7,
         scratch_shapes=[
             pltpu.VMEM((rows, width), F32), pltpu.VMEM((sk, rows), F32), pltpu.VMEM((1, PANEL), jnp.int32),
+            pltpu.VMEM((rows, PANEL), F32), square(2), square(2), tile(16),
             pltpu.VMEM((rows, PANEL), F32), square(), square(), square(),
             pltpu.VMEM((2, rows, PANEL), F32),
             part(2 * NY), part(2 * NY), part(), part(NZX), part(), part(2 * NY),
@@ -506,15 +520,15 @@
             flat(1, sk, width), flat(1, rows, PANEL), flat(1, PANEL, width),
             flat(1, PANEL, PANEL), flat(rows, width),
         ),
-        in_specs=[VMEM_SPEC] * 6,
+        in_specs=[VMEM_SPEC] * 7,
         out_specs=(hbm,) * 5,
         scratch_shapes=[
             pltpu.VMEM((sk, width), F32), pltpu.VMEM((rows, PANEL), F32), pltpu.VMEM((PANEL, width), F32),
-            pltpu.VMEM((PANEL, PANEL), F32), pltpu.VMEM((rows, width), F32), dma((11,)),
+            pltpu.VMEM((rows, width), F32), dma((11,)),
         ],
         compiler_params=pltpu.CompilerParams(vmem_limit_bytes=VMEM_UPDATE),
         name="update",
-    )(swapped, panel, inner, sketches, factors, inverses)
+    )(*mid)
 
 
 def solution(mesh):

time: 46.2 us -> 45.4 us (0.983)
  Pallas kernels: 45.5 us -> 44.7 us
    pallas_call x1, Pallas kernels: 43.2 us -> 42.7 us  [shards(): pl.pallas_call(reduce_kernel, out_shape=(flat(rows, width), flat(rows, PA...]
where the time goes in v10:
time: 45.4 us; the launch traced here: 45.3 us
  Pallas kernels  44.7 us (98%)
  between operations  0.64 us (1%)
    pallas_call x1, Pallas kernels, shards(): pl.pallas_call(reduce_kernel, out_shape=(flat(rows, width), flat(rows, PA...  42.7 us
    pallas_call x1, Pallas kernels, shards(): pl.pallas_call(update_kernel, out_shape=(flat(1, sk, width), flat(1, rows...  1.98 us

profile of v10, /device:TPU:1, one launch (start us, length us, event | category | flops | bytes accessed | tf_op | source)
XLA Modules:
  0.0 45.3 jit_solution(7431122295226910724)
XLA Ops:
  0.6 42.7 %reduce.1 = (f32[256,512]{1,0:T(8,128)S(1)}, f32[256,128]{1,0:T(8,128)S(1)}, f32[4,128,128]{2,1,0:T(8,128)S(1)}, f32[4,16,9,128]{3,2,1,0:T(8,128)S(1)}, f32[128,...) custom-call(f32[256,512]{1,0:T(8,128)} %slab_hbm.1, f32[144,256]{1,0:T(8,128)} %sketch_hbm.1, ...), custom_call_target="tpu_custom_call" | custom-call | tf_op jit(solution)/shard_map/reduce/pallas_call | solution.py:492
  43.3 2.0 %update.1 = (f32[1,144,512]{2,1,0:T(8,128)}, f32[1,256,128]{2,1,0:T(8,128)}, f32[1,128,512]{2,1,0:T(8,128)}, f32[1,128,128]{2,1,0:T(8,128)}, f32[256,512]{1,0:T(8,128)}) custom-call(f32[256,512]{1,0:T(8,128)S(1)} %get-tuple-element.12.b_ref, f32[256,128]{1,0:T(8,128)S(1)} %get-tuple-element.13.q_ref, f32[4,128,128]{2,1,0:T(8,128)S(1)} %get-tuple-element.14.g_ref, ...), custom_call_target="tpu_custom_call" | custom-call | tf_op jit(solution)/shard_map/update/pallas_call | solution.py:517

commit v11 on v10

--- a/solution.py
+++ b/solution.py
@@ -138,10 +138,19 @@
     load_slab.start()
     load_sketch.start()
 
-    y_peers = [(lax.rem(y + i, NY), i) for i in range(1, NY)]
-    zx_peers = [lax.rem(w + i, NZX) for i in range(1, NZX)]
+    ring = lambda d, n: min(d, n - d)
+    z, x = lax.div(w, 2), lax.rem(w, 2)
+    zx_at = lambda dz, dx: lax.rem(z + dz, NZX // 2) * 2 + (1 - x if dx else x)
+    by_hops = lambda offsets: sorted(offsets, key=lambda o: -(ring(o[0], NY) + ring(o[1], NZX // 2) + 2 * o[2]))
+    y_peers = [(lax.rem(y + dy, NY), dy) for dy in (2, 1, 3)]
+    zx_offsets = by_hops([(0, dz, dx) for dz in range(NZX // 2) for dx in range(2) if dz or dx])
+    zx_peers = [zx_at(dz, dx) for _, dz, dx in zx_offsets]
+    all_offsets = by_hops(
+        [(dy, dz, dx) for dy in range(NY) for dz in range(NZX // 2) for dx in range(2) if dy or dz or dx]
+    )
+    row_peers = [(lax.rem(y + dy, NY), zx_at(dz, dx)) for dy, dz, dx in all_offsets]
     own = y * 2 + core
-    pair_peers = [lax.rem(own + i, 2 * NY) for i in range(1, 2 * NY)]
+    pair_peers = [lax.rem(own + i, 2 * NY) for i in (4, 3, 5, 2, 6, 1, 7)]
 
     def pair_device(t):
         return (lax.div(t, 2) * NZX + w, c - core + lax.rem(t, 2))
@@ -283,15 +292,15 @@
     to_zx(lambda t: gsum.at[tile(t)], lambda m: gb.at[m], gb_sem)
     gb[w] = gsum[tile(w)]
 
-    from_zx(lambda t: sb.at[t], sb_sem)
-    sfull[y, w] = total_of(sb, NZX)
-    to_zx(lambda t: sfull.at[y, w], lambda m: sfull.at[y, m], sc_sem)
-
     from_zx(lambda t: wb.at[t], wb_sem)
     wtot[...] = two_float_total(wb, NZX)
     for t in pair_peers:
         send(wtot, wfull.at[own], wc_sem.at[0, t], wc_sem.at[1, own], pair_device(t))
     wfull[own] = wtot[...]
+
+    from_zx(lambda t: sb.at[t], sb_sem)
+    sfull[y, w] = total_of(sb, NZX)
+    to_zx(lambda t: sfull.at[y, w], lambda m: sfull.at[y, m], sc_sem)
 
     for t in pair_peers:
         remote(wfull.at[t], wfull.at[t], wc_sem.at[0, t], wc_sem.at[1, t], (r, c)).wait_recv()
@@ -302,15 +311,15 @@
 
     from_zx(lambda t: gb.at[t], gb_sem)
     gfull[y, tile(w)] = total_of(gb, NZX)
-    row_peers = [lax.rem(r + i, NY * NZX) for i in range(1, NY * NZX)]
-    for t in row_peers:
+    for ty, tw in row_peers:
+        t = ty * NZX + tw
         send(gfull.at[y, tile(w)], gfull.at[y, tile(w)], gc_sem.at[0, t], gc_sem.at[1, r], (t, c))
 
     def sketch_home():
         from_zx(lambda t: sfull.at[y, t], sc_sem)
         to_y(lambda t: sfull.at[y], lambda m: sfull.at[m], sd_sem)
 
-    eliminate(high, r_out.at[0], x_out.at[0], held, {4: sketch_home})
+    eliminate(high, r_out.at[0], x_out.at[0], held, {8: sketch_home})
     r_one = r_out[0]
     x_one = x_out[0]
 
@@ -330,8 +339,9 @@
     rfac_ref[...] = hdot(r_out[1], r_out[0])
 
     from_y(lambda t: sfull.at[t], sd_sem)
-    for t in row_peers:
-        piece = gfull.at[lax.div(t, NZX), tile(lax.rem(t, NZX))]
+    for ty, tw in row_peers:
+        t = ty * NZX + tw
+        piece = gfull.at[ty, tile(tw)]
         remote(piece, piece, gc_sem.at[0, t], gc_sem.at[1, t], (r, c)).wait_recv()
     for copy in pending:
         copy.wait_send()

time: 45.4 us -> 45.3 us (level)
  no operation moved by 1% of the time
where the time goes in v11:
time: 45.3 us; the launch traced here: 45.2 us
  Pallas kernels  44.5 us (98%)
  between operations  0.64 us (1%)
    pallas_call x1, Pallas kernels, shards(): pl.pallas_call(reduce_kernel, out_shape=(flat(rows, width), flat(rows, PA...  42.5 us
    pallas_call x1, Pallas kernels, shards(): pl.pallas_call(update_kernel, out_shape=(flat(1, sk, width), flat(1, rows...  1.98 us

profile of v11, /device:TPU:1, one launch (start us, length us, event | category | flops | bytes accessed | tf_op | source)
XLA Modules:
  0.0 45.2 jit_solution(4000958009789457534)
XLA Ops:
  0.6 42.5 %reduce.1 = (f32[256,512]{1,0:T(8,128)S(1)}, f32[256,128]{1,0:T(8,128)S(1)}, f32[4,128,128]{2,1,0:T(8,128)S(1)}, f32[4,16,9,128]{3,2,1,0:T(8,128)S(1)}, f32[128,...) custom-call(f32[256,512]{1,0:T(8,128)} %slab_hbm.1, f32[144,256]{1,0:T(8,128)} %sketch_hbm.1, ...), custom_call_target="tpu_custom_call" | custom-call | tf_op jit(solution)/shard_map/reduce/pallas_call | solution.py:502
  43.2 2.0 %update.1 = (f32[1,144,512]{2,1,0:T(8,128)}, f32[1,256,128]{2,1,0:T(8,128)}, f32[1,128,512]{2,1,0:T(8,128)}, f32[1,128,128]{2,1,0:T(8,128)}, f32[256,512]{1,0:T(8,128)}) custom-call(f32[256,512]{1,0:T(8,128)S(1)} %get-tuple-element.12.b_ref, f32[256,128]{1,0:T(8,128)S(1)} %get-tuple-element.13.q_ref, f32[4,128,128]{2,1,0:T(8,128)S(1)} %get-tuple-element.14.g_ref, ...), custom_call_target="tpu_custom_call" | custom-call | tf_op jit(solution)/shard_map/update/pallas_call | solution.py:527

commit v12 on v11

--- a/solution.py
+++ b/solution.py
@@ -114,12 +114,12 @@
 
 def reduce_kernel(
     slab_hbm, sketch_hbm, piv_hbm,
-    b_ref, q_ref, gfull, sfull, first_ref, rfac_ref, inv_ref,
+    b_ref, q_ref, gfull, s_ref, first_ref, rfac_ref, inv_ref, panel_ref,
     slab_ref, sketch_ref, piv_ref, p_ref, r_out, x_out, held,
     pk, pp, rc1, rc2, leadbuf,
     wpart, wa, wsum, wb, wtot, wfull,
     gpart, ga, gsum, gb,
-    spart, sa, ssum, sb,
+    spart, sa, ssum, sb, sfull,
     sem_in, sem1, sem_p, sem_lead, wa_sem, wb_sem, wc_sem, ga_sem, gb_sem, gc_sem,
     sa_sem, sb_sem, sc_sem, sd_sem, relay,
 ):
@@ -334,11 +334,16 @@
 
     inverse = hdot(x_out[1], x_out[0])
     inv_ref[...] = inverse
-    q_ref[...] = hdot(p_ref[...], inverse, (1, 1))
+    basis = hdot(p_ref[...], inverse, (1, 1))
+    q_ref[...] = basis
+    panel_ref[...] = basis * 128.0
     first_ref[...] = r_out[0] * (1.0 / 128.0)
     rfac_ref[...] = hdot(r_out[1], r_out[0])
 
     from_y(lambda t: sfull.at[t], sd_sem)
+    for k in range(NY):
+        for t in range(NZX):
+            s_ref[9 * t : 9 * t + 9, 128 * k : 128 * k + 128] = sfull[k, t]
     for ty, tw in row_peers:
         t = ty * NZX + tw
         piece = gfull.at[ty, tile(tw)]
@@ -382,7 +387,7 @@
 def block_factor(v, columns, held, first, sub, lane):
     slot = first % 16
     for i in range(8):
-        held[slot + i] = columns[i]
+        held[slot + i, 0:8] = columns[i]
     a = {(i, j): held[slot + i, pl.ds(j, 8, stride=0), :] for j in range(8) for i in range(j + 1)}
     m = [[None] * 8 for _ in range(8)]
     for i in range(8):
@@ -450,9 +455,9 @@
 
 
 def update_kernel(
-    b_ref, q_ref, g_ref, s_ref, first_ref, rfac_ref, inv_ref,
+    b_ref, q_ref, g_ref, s_ref, first_ref, rfac_ref, inv_ref, panel_ref,
     s_hbm, q_hbm, e_hbm, first_hbm, out_hbm,
-    sbuf, qbuf, ebuf, obuf, sem,
+    ebuf, obuf, sem,
 ):
     lead_block = lax.axis_index("col") == 0
     copies = []
@@ -463,27 +468,25 @@
         copy.start()
         copies.append(copy)
 
-    for k in range(4):
-        for t in range(NZX):
-            sbuf[9 * t : 9 * t + 9, 128 * k : 128 * k + 128] = s_ref[k, t]
-    store(0, sbuf, s_hbm.at[0])
-    store(8, first_ref, first_hbm.at[0])
+    store(0, s_ref, s_hbm.at[0])
+    store(1, first_ref, first_hbm.at[0])
+    store(2, panel_ref, q_hbm.at[0])
     basis = q_ref[...]
-    qbuf[...] = basis * 128.0
-    store(9, qbuf, q_hbm.at[0])
     r_factor = rfac_ref[...]
     inverse = inv_ref[...]
-    for k in range(4):
-        cols = slice(128 * k, 128 * k + 128)
-        projected = hdot(inverse, g_ref[k])
+    for k in range(2):
+        cols = slice(256 * k, 256 * k + 256)
+        projected = hdot(inverse, jnp.concatenate([g_ref[2 * k], g_ref[2 * k + 1]], axis=1))
         rest = b_ref[:, cols] - hdot(basis, projected)
         if k == 0:
-            projected = jnp.where(lead_block, r_factor, projected)
-            rest = jnp.where(lead_block, 0.0, rest)
+            head = jnp.where(lead_block, r_factor, projected[:, :PANEL])
+            projected = jnp.concatenate([head, projected[:, PANEL:]], axis=1)
+            head = jnp.where(lead_block, 0.0, rest[:, :PANEL])
+            rest = jnp.concatenate([head, rest[:, PANEL:]], axis=1)
         ebuf[:, cols] = projected * scale
         obuf[:, cols] = rest
-        store(4 + k, obuf.at[:, cols], out_hbm.at[:, cols])
-    store(10, ebuf, e_hbm.at[0])
+        store(3 + 2 * k, ebuf.at[:, cols], e_hbm.at[0, :, cols])
+        store(4 + 2 * k, obuf.at[:, cols], out_hbm.at[:, cols])
     for copy in copies:
         copy.wait()
 
@@ -502,19 +505,19 @@
     mid = pl.pallas_call(
         reduce_kernel,
         out_shape=(
-            flat(rows, width), flat(rows, PANEL), flat(4, PANEL, PANEL), flat(4, NZX, sk // NZX, PANEL),
-            flat(PANEL, PANEL), flat(PANEL, PANEL), flat(PANEL, PANEL),
+            flat(rows, width), flat(rows, PANEL), flat(4, PANEL, PANEL), flat(sk, width),
+            flat(PANEL, PANEL), flat(PANEL, PANEL), flat(PANEL, PANEL), flat(rows, PANEL),
         ),
         in_specs=[hbm] * 3,
-        out_specs=(VMEM_SPEC,) * 7,
+        out_specs=(VMEM_SPEC,) * 8,
         scratch_shapes=[
             pltpu.VMEM((rows, width), F32), pltpu.VMEM((sk, rows), F32), pltpu.VMEM((1, PANEL), jnp.int32),
-            pltpu.VMEM((rows, PANEL), F32), square(2), square(2), tile(16),
+            pltpu.VMEM((rows, PANEL), F32), square(2), square(2), pltpu.VMEM((16, 16, 128), F32),
             pltpu.VMEM((rows, PANEL), F32), square(), square(), square(),
             pltpu.VMEM((2, rows, PANEL), F32),
             part(2 * NY), part(2 * NY), part(), part(NZX), part(), part(2 * NY),
             square(NY), square(NY), square(), tile(NZX),
-            tall(NY), tall(NY), nine(NZX), nine(NZX),
+            tall(NY), tall(NY), nine(NZX), nine(NZX), nine(NY, NZX),
             dma((3,)), dma((4,)), dma((2,)), dma((4,)), dma((2, 2 * NY)), dma((2, NZX)), dma((2, 2 * NY)),
             dma((2, NY)), dma((2, NZX)), dma((2, NY * NZX)),
             dma((2, NY)), dma((2, NZX)), dma((2, NZX)), dma((2, NY)), pltpu.SemaphoreType.REGULAR((2,)),
@@ -530,11 +533,10 @@
             flat(1, sk, width), flat(1, rows, PANEL), flat(1, PANEL, width),
             flat(1, PANEL, PANEL), flat(rows, width),
         ),
-        in_specs=[VMEM_SPEC] * 7,
+        in_specs=[VMEM_SPEC] * 8,
         out_specs=(hbm,) * 5,
         scratch_shapes=[
-            pltpu.VMEM((sk, width), F32), pltpu.VMEM((rows, PANEL), F32), pltpu.VMEM((PANEL, width), F32),
-            pltpu.VMEM((rows, width), F32), dma((11,)),
+            pltpu.VMEM((PANEL, width), F32), pltpu.VMEM((rows, width), F32), dma((7,)),
         ],
         compiler_params=pltpu.CompilerParams(vmem_limit_bytes=VMEM_UPDATE),
         name="update",

time: 45.3 us -> 45.2 us (level)
  no operation moved by 1% of the time
where the time goes in v12:
time: 45.2 us; the launch traced here: 45.1 us
  Pallas kernels  44.5 us (98%)
  between operations  0.64 us (1%)
    pallas_call x1, Pallas kernels, shards(): pl.pallas_call(reduce_kernel, out_shape=(flat(rows, width), flat(rows, PA...  42.6 us
    pallas_call x1, Pallas kernels, shards(): pl.pallas_call(update_kernel, out_shape=(flat(1, sk, width), flat(1, rows...  1.83 us

profile of v12, /device:TPU:1, one launch (start us, length us, event | category | flops | bytes accessed | tf_op | source)
XLA Modules:
  0.0 45.1 jit_solution(352023515487998203)
XLA Ops:
  0.6 42.6 %reduce.1 = (f32[256,512]{1,0:T(8,128)S(1)}, f32[256,128]{1,0:T(8,128)S(1)}, f32[4,128,128]{2,1,0:T(8,128)S(1)}, f32[144,512]{1,0:T(8,128)S(1)}, f32[128,128]{1,...) custom-call(f32[256,512]{1,0:T(8,128)} %slab_hbm.1, ...), custom_call_target="tpu_custom_call" | custom-call | tf_op jit(solution)/shard_map/reduce/pallas_call | solution.py:505
  43.3 1.8 %update.1 = (f32[1,144,512]{2,1,0:T(8,128)}, f32[1,256,128]{2,1,0:T(8,128)}, f32[1,128,512]{2,1,0:T(8,128)}, f32[1,128,128]{2,1,0:T(8,128)}, f32[256,512]{1,0:T(8,128)}) custom-call(f32[256,512]{1,0:T(8,128)S(1)} %get-tuple-element.13.b_ref, f32[256,128]{1,0:T(8,128)S(1)} %get-tuple-element.14.q_ref, f32[4,128,128]{2,1,0:T(8,128)S(1)} %get-tuple-element.15.g_ref, ...), custom_call_target="tpu_custom_call" | custom-call | tf_op jit(solution)/shard_map/update/pallas_call | solution.py:530

commit v13 on v12

--- a/solution.py
+++ b/solution.py
@@ -304,16 +304,16 @@
 
     for t in pair_peers:
         remote(wfull.at[t], wfull.at[t], wc_sem.at[0, t], wc_sem.at[1, t], (r, c)).wait_recv()
-    packed = jnp.concatenate([wfull[o, 0:16] for o in range(2 * NY)], axis=0)
-    diagonal = wfull[0, 16:17]
-    high = unpack_symmetric(packed, diagonal)
-    low = unpack_symmetric(pltpu.roll(packed, 64, 1), pltpu.roll(diagonal, 64, 1))
-
     from_zx(lambda t: gb.at[t], gb_sem)
     gfull[y, tile(w)] = total_of(gb, NZX)
     for ty, tw in row_peers:
         t = ty * NZX + tw
         send(gfull.at[y, tile(w)], gfull.at[y, tile(w)], gc_sem.at[0, t], gc_sem.at[1, r], (t, c))
+
+    packed = jnp.concatenate([wfull[o, 0:16] for o in range(2 * NY)], axis=0)
+    diagonal = wfull[0, 16:17]
+    high = unpack_symmetric(packed, diagonal)
+    low = unpack_symmetric(pltpu.roll(packed, 64, 1), pltpu.roll(diagonal, 64, 1))
 
     def sketch_home():
         from_zx(lambda t: sfull.at[y, t], sc_sem)

time: 45.2 us -> 45 us (level)
  no operation moved by 1% of the time
where the time goes in v13:
time: 45 us; the launch traced here: 44.9 us
  Pallas kernels  44.3 us (98%)
  between operations  0.64 us (1%)
    pallas_call x1, Pallas kernels, shards(): pl.pallas_call(reduce_kernel, out_shape=(flat(rows, width), flat(rows, PA...  42.4 us
    pallas_call x1, Pallas kernels, shards(): pl.pallas_call(update_kernel, out_shape=(flat(1, sk, width), flat(1, rows...  1.83 us

profile of v13, /device:TPU:1, one launch (start us, length us, event | category | flops | bytes accessed | tf_op | source)
XLA Modules:
  0.0 44.9 jit_solution(3182785289025051491)
XLA Ops:
  0.6 42.4 %reduce.1 = (f32[256,512]{1,0:T(8,128)S(1)}, f32[256,128]{1,0:T(8,128)S(1)}, f32[4,128,128]{2,1,0:T(8,128)S(1)}, f32[144,512]{1,0:T(8,128)S(1)}, f32[128,128]{1,...) custom-call(f32[256,512]{1,0:T(8,128)} %slab_hbm.1, ...), custom_call_target="tpu_custom_call" | custom-call | tf_op jit(solution)/shard_map/reduce/pallas_call | solution.py:505
  43.1 1.8 %update.1 = (f32[1,144,512]{2,1,0:T(8,128)}, f32[1,256,128]{2,1,0:T(8,128)}, f32[1,128,512]{2,1,0:T(8,128)}, f32[1,128,128]{2,1,0:T(8,128)}, f32[256,512]{1,0:T(8,128)}) custom-call(f32[256,512]{1,0:T(8,128)S(1)} %get-tuple-element.13.b_ref, f32[256,128]{1,0:T(8,128)S(1)} %get-tuple-element.14.q_ref, f32[4,128,128]{2,1,0:T(8,128)S(1)} %get-tuple-element.15.g_ref, ...), custom_call_target="tpu_custom_call" | custom-call | tf_op jit(solution)/shard_map/update/pallas_call | solution.py:530
